TPU v7x, 128 devices: a whole 4x4x4 slice. The times are simulated.
128 devices in a mesh: mem: 8 (over x, core), tile: 16 (over y, z).
Axes of the slice: x: 4, y: 4, z: 4, core: 2. Of those that a mesh axis runs over, the one named last changes fastest.
Arguments:
- control: float32 [16, 64, 320, 160], P('mem', None, 'tile'), may hold values from -6 to 6
- ens_perts: float32 [16, 2, 64, 320, 160], P('mem', None, None, 'tile'), may hold values from -8 to 8
- vert_corr: float32 [64, 64], replicated, may hold values from -0.75 to 0.75
- slab_wts: float32 [16, 4], replicated, may hold values from 0.25 to 2
- level_slab: int32 [64], replicated, may hold values from 0 to 15, as said below
Outputs:
- wind_share: float32 [2, 64, 320, 160], P(None, 'mem', 'tile')
- gradient: float32 [16, 64, 320, 160], P('mem', None, 'tile')
Inputs may be any that keep to these rules, and one draw needn't show every extreme that they name: `level_slab`: each slab holds a contiguous run of levels and slab numbers never fall with the level; every slab holds 1 to 8 levels, and one slab holds exactly 8.
All inputs are finite; a program needn't handle non-finite values.
Results may differ from a plain program's by a relative error of at most 0.0001.
Values sent between devices are 32-bit elements; how exact they have to be, the bound alone decides.
No kernel may reach another device: no remote copies, remote signals or barrier semaphores. Data moves between devices by JAX's collectives and lax.ppermute only.
A program may use at most 128 MiB of HBM per device.

v0:
```python
import math

import jax
import jax.numpy as jnp
from jax import lax
from jax.sharding import PartitionSpec as P

dilation_steps = (1, 2, 4, 8)
highest = lax.Precision.HIGHEST


def line_filter(length, dilation):
    positions = jnp.arange(length)
    distance = jnp.abs(positions[None, :] - positions[:, None])
    inside = (distance % dilation == 0) & (distance <= 6 * dilation)
    ratio = (distance // dilation).astype(jnp.float32)
    kernel = jnp.where(inside, jnp.exp(-ratio * ratio / 8.0), 0.0)
    cubed = jnp.dot(jnp.dot(kernel, kernel, precision=highest), kernel, precision=highest)
    centre = cubed[:, length // 2]
    return cubed / jnp.sqrt(jnp.sum(centre * centre))


def horizontal(fields, weights, filters):
    running = jnp.zeros(fields.shape, jnp.float32)
    for scale_num in range(len(filters)):
        along_x, along_y = filters[scale_num]
        stepped = jnp.einsum("ij,...jy->...iy", along_x, fields, precision=highest)
        stepped = jnp.einsum("...iy,ly->...il", stepped, along_y, precision=highest)
        running = running + weights[:, scale_num][:, None, None] * stepped
    return running


def regroup_apply(data_in, level_slab, slab_wts, filters):
    members, levels, rows_tile, cols_all = data_in.shape
    tile_count = lax.axis_size("tile")
    my_tile = lax.axis_index("tile")
    capacity = 2 * levels // tile_count
    slab_ids = jnp.arange(tile_count)
    member_of = (level_slab[:, None] == slab_ids[None, :]).astype(jnp.int32)
    counts = jnp.sum(member_of, axis=0)
    starts = jnp.cumsum(counts) - counts
    slot_ids = jnp.arange(capacity)
    slot_level = starts[:, None] + slot_ids[None, :]
    slot_level = jnp.where(slot_ids[None, :] < counts[:, None], slot_level, 0)
    packed = jnp.take(data_in, slot_level.reshape(-1), axis=1)
    packed = packed.reshape(members, tile_count, capacity, rows_tile, cols_all)
    own_weights = lax.dynamic_index_in_dim(slab_wts, my_tile, 0, keepdims=False)
    weights = jnp.broadcast_to(own_weights[None, :], (capacity, own_weights.shape[0]))
    smooth = horizontal(
        lax.all_to_all(packed, "tile", split_axis=1, concat_axis=3, tiled=True), weights, filters
    )
    returned = lax.all_to_all(smooth, "tile", split_axis=3, concat_axis=1, tiled=True)
    level_rank = jnp.arange(levels) - jnp.sum(member_of * starts[None, :], axis=1)
    position = level_slab * capacity + level_rank
    flat_slots = returned.reshape(members, tile_count * capacity, rows_tile, cols_all)
    result_levels = jnp.take(flat_slots, position, axis=1)
    return result_levels


def shards(control, ens_perts, vert_corr, slab_wts, level_slab):
    members, levels, rows_tile, cols_all = control.shape
    tile_count = lax.axis_size("tile")
    rows_all = rows_tile * tile_count
    mem_count = lax.axis_size("mem")
    member_scale = 1.0 / math.sqrt(members * mem_count - 1)
    filters = [
        (line_filter(rows_all, dilation), line_filter(cols_all, dilation))
        for dilation in dilation_steps
    ]
    smooth = regroup_apply(control, level_slab, slab_wts, filters)
    localized = jnp.einsum("lm,bmxy->blxy", vert_corr, smooth, precision=highest)
    partial_wind = jnp.einsum("bclxy,blxy->clxy", ens_perts, localized, precision=highest)
    wind_full = lax.psum(partial_wind, "mem") * member_scale
    level_share = levels // mem_count
    wind_share = lax.dynamic_slice_in_dim(
        wind_full, lax.axis_index("mem") * level_share, level_share, 1
    )
    adjoint = jnp.sum(ens_perts * wind_full[None], axis=1) * member_scale
    adjoint = jnp.einsum("ml,bmxy->blxy", vert_corr, adjoint, precision=highest)
    filtered_back = regroup_apply(adjoint, level_slab, slab_wts, filters)
    return (wind_share, control + filtered_back)


def solution(mesh):
    return jax.shard_map(
        shards,
        mesh=mesh,
        in_specs=(P("mem", None, "tile", None), P("mem", None, None, "tile", None), P(), P(), P()),
        out_specs=(P(None, "mem", "tile", None), P("mem", None, "tile", None)),
        check_vma=False,
    )
```

profile of v0, /device:TPU:116, one launch (start us, length us, event | category | flops | bytes accessed | tf_op | source)
XLA Modules:
  0.0 661.9 jit_solution(16314944566816116443)
XLA Ops:
  8.4 12.5 %gather_fusion = f32[128,2,20,160]{3,0,2,1:T(8,128)} fusion(f32[2,64,20,160]{3,1,2,0:T(8,128)} %param.9, s32[1024]{0:T(1024)S(1)} %pad_clamp_fusion.1), kind=kCustom, calls=%fused_computation.clone | custom fusion | bytes 6554112 | tf_op jit(solution)/shard_map/jit(_take)/gather | solution.py:45
  26.9 7.1 %all-to-all-start = ((f32[2,16,8,20,160]{4,2,3,0,1:T(8,128)}), f32[2,16,8,20,160]{4,2,3,0,1:T(8,128)}, u32[]{:S(2)}, u32[]{:S(2)}) async-start(f32[2,16,8,20,160]{4,2,3,0,1:T(8,128)} %copy.144), calls=%async_computation | async-start | bytes 10485760 | tf_op jit(solution)/shard_map/all_to_all | solution.py:50
  59.7 58.6 %all-to-all-done = f32[2,16,8,20,160]{4,2,3,0,1:T(8,128)} async-done(((f32[2,16,8,20,160]{4,2,3,0,1:T(8,128)}), f32[2,16,8,20,160]{4,2,3,0,1:T(8,128)}, u32[]{:S(2)}, u32[]{:S(2)}) %all-to-all-start) | async-done | bytes 3276832 | tf_op jit(solution)/shard_map/all_to_all | solution.py:50
  118.4 5.4 copy.145
  123.7 5.6 copy.146
  129.3 10.6 %fusion.51 = f32[2,8,160,320]{3,2,1,0:T(8,128)S(1)} fusion(f32[2,8,320,160]{2,3,1,0:T(8,128)} %copy.146, f32[320,320]{0,1:T(8,128)S(1)} %fusion.92, f32[]{:T(128)S(6)} %sqrt.30), kind=kOutput, calls=%fused_computation.75 | convolution fusion | flops 3145830400 | bytes 6963204 | tf_op jit(solution)/shard_map/ij,...jy->...iy/dot_general | solution.py:27
  139.9 8.5 %fusion.55 = f32[2,8,160,320]{3,2,1,0:T(8,128)S(1)} fusion(f32[2,8,320,160]{2,3,1,0:T(8,128)S(1)} %copy-done.4, f32[320,320]{0,1:T(8,128)S(1)} %fusion.96, f32[]{:T(128)S(6)} %sqrt.28), kind=kOutput, calls=%fused_computation.79 | convolution fusion | flops 3145830400 | bytes 6963204 | tf_op jit(solution)/shard_map/ij,...jy->...iy/dot_general | solution.py:27
  148.4 8.3 %fusion.59 = f32[2,8,160,320]{3,2,1,0:T(8,128)S(1)} fusion(f32[2,8,320,160]{2,3,1,0:T(8,128)S(1)} %copy-done.4, f32[320,320]{0,1:T(8,128)S(1)} %fusion.100, f32[]{:T(128)S(6)} %sqrt.26), kind=kOutput, calls=%fused_computation.83 | convolution fusion | flops 3145830400 | bytes 6963204 | tf_op jit(solution)/shard_map/ij,...jy->...iy/dot_general | solution.py:27
  156.8 8.6 %fusion.63 = f32[2,8,160,320]{3,2,1,0:T(8,128)S(1)} fusion(f32[2,8,320,160]{2,3,1,0:T(8,128)S(1)} %copy-done.4, f32[320,320]{0,1:T(8,128)S(1)} %fusion.76, f32[]{:T(128)S(6)} %sqrt.24), kind=kOutput, calls=%fused_computation.87 | convolution fusion | flops 3145830400 | bytes 6963204 | tf_op jit(solution)/shard_map/ij,...jy->...iy/dot_general | solution.py:27
  177.7 9.4 %add_bitcast_fusion.1 = f32[2,1,8,320,160]{3,4,2,0,1:T(8,128)} fusion(f32[2,8,320,160]{2,3,1,0:T(8,128)S(1)} %fusion.8, f32[2,8,320,160]{2,3,1,0:T(8,128)S(1)} %fusion.10, f32[2,8,320,160]{2,3,1,0:T(8,128)S(1)} %fusion.12, f32[2,8,160,320]{3,2,1,0:T(8,128)S(1)} %fusion.63, f32[]{:T(128)} %bitcast.26, f32[]{:T(128)} %bitcast.20, f32[]{:T(128)} %bitcast.14, ...), kind=kOutput, calls=%fused_computation.27 | convolution fusion | flops 1578624000 | bytes 16486420 | tf_op jit(solution)/shard_map/...iy,ly->...il/dot_general | solution.py:28
  187.0 6.3 copy.158
  193.4 7.1 %all-to-all-start.1 = ((f32[2,1,8,320,160]{4,2,0,1,3:T(8,128)}), f32[2,1,8,320,160]{4,2,0,1,3:T(8,128)}, u32[]{:S(2)}, u32[]{:S(2)}) async-start(f32[2,1,8,320,160]{4,2,0,1,3:T(8,128)} %copy.158), calls=%async_computation.1 | async-start | bytes 10485760 | tf_op jit(solution)/shard_map/all_to_all | solution.py:52
  200.8 75.0 %all-to-all-done.1 = f32[2,1,8,320,160]{4,2,0,1,3:T(8,128)} async-done(((f32[2,1,8,320,160]{4,2,0,1,3:T(8,128)}), f32[2,1,8,320,160]{4,2,0,1,3:T(8,128)}, u32[]{:S(2)}, u32[]{:S(2)}) %all-to-all-start.1) | async-done | bytes 3276832 | tf_op jit(solution)/shard_map/all_to_all | solution.py:52
  279.2 6.4 copy.161
  285.6 7.2 %gather_fusion.1 = f32[64,2,20,160]{3,1,2,0:T(2,128)} fusion(f32[2,128,20,160]{3,0,2,1:T(2,128)} %copy.161, s32[1024]{0:T(1024)S(1)} %pad_clamp_fusion), kind=kCustom, calls=%fused_computation.1.clone | custom fusion | bytes 3277056 | tf_op jit(solution)/shard_map/jit(_take)/gather | solution.py:56
  302.2 64.5 %all-reduce.2.cloned.1.call-done = f32[2,64,20,160]{3,1,2,0:T(8,128)} async-done(((f32[2,64,20,160]{3,1,2,0:T(8,128)}), f32[2,64,20,160]{3,1,2,0:T(8,128)}) %all-reduce.2.cloned.1.call-update) | async-done | bytes 1638416 | tf_op jit(solution)/shard_map/psum | solution.py:73
  368.8 4.5 multiply_reduce_fusion.1
  378.1 10.7 %gather_fusion.2 = f32[128,2,20,160]{3,1,2,0:T(2,128)} fusion(f32[2,64,20,160]{3,0,2,1:T(2,128)S(1)} %copy.164, s32[1024]{0:T(1024)S(1)} %pad_clamp_fusion.1), kind=kCustom, calls=%fused_computation.2.clone | custom fusion | bytes 6554112 | tf_op jit(solution)/shard_map/jit(_take)/gather | solution.py:45
  388.8 5.8 broadcast_select_fusion
  396.2 66.3 %all_to_all.60 = f32[2,16,8,20,160]{4,2,3,0,1:T(8,128)S(1)} all-to-all(f32[2,16,8,20,160]{4,2,3,0,1:T(8,128)S(1)} %copy.165), channel_id=1, replica_groups=mesh['mem'=8,'tile'=16] {'tile'}, dimensions={1} | all-to-all | bytes 6553600 | tf_op jit(solution)/shard_map/all_to_all | solution.py:50
  465.2 5.8 copy.167
  471.0 10.6 %fusion.49 = f32[2,8,160,320]{3,2,1,0:T(8,128)S(1)} fusion(f32[2,8,320,160]{2,3,1,0:T(8,128)} %copy.167, f32[320,320]{0,1:T(8,128)S(1)} %fusion.92, f32[]{:T(128)S(6)} %sqrt.30), kind=kOutput, calls=%fused_computation.73 | convolution fusion | flops 3145830400 | bytes 6963204 | tf_op jit(solution)/shard_map/ij,...jy->...iy/dot_general | solution.py:27
  481.6 8.5 %fusion.53 = f32[2,8,160,320]{3,2,1,0:T(8,128)S(1)} fusion(f32[2,8,320,160]{2,3,1,0:T(8,128)S(1)} %copy-done.3, f32[320,320]{0,1:T(8,128)S(1)} %copy-done.7, f32[]{:T(128)S(6)} %sqrt.28), kind=kOutput, calls=%fused_computation.77 | convolution fusion | flops 3145830400 | bytes 6963204 | tf_op jit(solution)/shard_map/ij,...jy->...iy/dot_general | solution.py:27
  490.2 8.3 %fusion.57 = f32[2,8,160,320]{3,2,1,0:T(8,128)S(1)} fusion(f32[2,8,320,160]{2,3,1,0:T(8,128)S(1)} %copy-done.3, f32[320,320]{0,1:T(8,128)S(1)} %copy-done.9, f32[]{:T(128)S(6)} %sqrt.26), kind=kOutput, calls=%fused_computation.81 | convolution fusion | flops 3145830400 | bytes 6963204 | tf_op jit(solution)/shard_map/ij,...jy->...iy/dot_general | solution.py:27
  498.5 8.8 %fusion.61 = f32[2,8,160,320]{3,2,1,0:T(8,128)S(1)} fusion(f32[2,8,320,160]{2,3,1,0:T(8,128)S(1)} %copy-done.3, f32[320,320]{0,1:T(8,128)S(1)} %copy-done.11, f32[]{:T(128)S(6)} %sqrt.24), kind=kOutput, calls=%fused_computation.85 | convolution fusion | flops 3145830400 | bytes 6963204 | tf_op jit(solution)/shard_map/ij,...jy->...iy/dot_general | solution.py:27
  519.4 9.4 %add_bitcast_fusion = f32[2,1,8,320,160]{3,4,2,0,1:T(8,128)} fusion(f32[2,8,320,160]{2,3,1,0:T(8,128)S(1)} %fusion, f32[2,8,320,160]{2,3,1,0:T(8,128)S(1)} %fusion.2, f32[2,8,320,160]{2,3,1,0:T(8,128)S(1)} %fusion.4, f32[2,8,160,320]{3,2,1,0:T(8,128)S(1)} %fusion.61, f32[]{:T(128)} %bitcast.26, f32[]{:T(128)} %bitcast.20, f32[]{:T(128)} %bitcast.14, ...), kind=kOutput, calls=%fused_computation.26 | convolution fusion | flops 1578624000 | bytes 16486420 | tf_op jit(solution)/shard_map/...iy,ly->...il/dot_general | solution.py:28
  528.8 6.3 copy.179
  535.1 8.6 %all-to-all-start.3 = ((f32[2,1,8,320,160]{4,2,0,1,3:T(8,128)}), f32[2,1,8,320,160]{4,2,0,1,3:T(8,128)}, u32[]{:S(2)}, u32[]{:S(2)}) async-start(f32[2,1,8,320,160]{4,2,0,1,3:T(8,128)} %copy.179), calls=%async_computation.3 | async-start | bytes 10485760 | tf_op jit(solution)/shard_map/all_to_all | solution.py:52
  545.5 85.3 %all-to-all-done.3 = f32[2,1,8,320,160]{4,2,0,1,3:T(8,128)} async-done(((f32[2,1,8,320,160]{4,2,0,1,3:T(8,128)}), f32[2,1,8,320,160]{4,2,0,1,3:T(8,128)}, u32[]{:S(2)}, u32[]{:S(2)}) %all-to-all-start.3) | async-done | bytes 3276832 | tf_op jit(solution)/shard_map/all_to_all | solution.py:52
  634.2 6.4 copy.182
  640.5 7.3 %gather_fusion.3 = f32[64,2,20,160]{3,1,2,0:T(2,128)} fusion(f32[2,128,20,160]{3,0,2,1:T(2,128)} %copy.182, s32[1024]{0:T(1024)S(1)} %pad_clamp_fusion), kind=kCustom, calls=%fused_computation.3.clone | custom fusion | bytes 3277056 | tf_op jit(solution)/shard_map/jit(_take)/gather | solution.py:56
  647.8 4.7 bitcast_add_fusion
  (104 shorter events, 83.1 us)
Async XLA Ops:
  7.2 289.0 %copy-start = (f32[64,64]{1,0:T(8,128)S(1)}, f32[64,64]{1,0:T(8,128)}, u32[]{:S(2)}) copy-start(f32[64,64]{1,0:T(8,128)} %param.11) | copy-start | bytes 49156
  26.9 91.5 %all-to-all-start = ((f32[2,16,8,20,160]{4,2,3,0,1:T(8,128)}), f32[2,16,8,20,160]{4,2,3,0,1:T(8,128)}, u32[]{:S(2)}, u32[]{:S(2)}) async-start(f32[2,16,8,20,160]{4,2,3,0,1:T(8,128)} %copy.144), calls=%async_computation | async-start | bytes 10485760 | tf_op jit(solution)/shard_map/all_to_all | solution.py:50
  42.9 97.1 %copy-start.6 = (f32[320,320]{0,1:T(8,128)}, f32[320,320]{0,1:T(8,128)S(1)}, u32[]{:S(2)}) copy-start(f32[320,320]{0,1:T(8,128)S(1)} %fusion.96) | copy-start | bytes 1228804
  45.2 124.1 %copy-start.12 = (f32[160,160]{0,1:T(8,128)}, f32[160,160]{0,1:T(8,128)S(1)}, u32[]{:S(2)}) copy-start(f32[160,160]{0,1:T(8,128)S(1)} %fusion.163) | copy-start | bytes 307204
  49.1 99.3 %copy-start.8 = (f32[320,320]{0,1:T(8,128)}, f32[320,320]{0,1:T(8,128)S(1)}, u32[]{:S(2)}) copy-start(f32[320,320]{0,1:T(8,128)S(1)} %fusion.100) | copy-start | bytes 1228804
  49.1 9.9 %copy-start.16 = (f32[16,4]{0,1:T(4,128)S(1)}, f32[16,4]{0,1:T(4,128)}, u32[]{:S(2)}) copy-start(f32[16,4]{0,1:T(4,128)} %param.12) | copy-start | bytes 772
  51.5 122.2 %copy-start.14 = (f32[160,160]{0,1:T(8,128)}, f32[160,160]{0,1:T(8,128)S(1)}, u32[]{:S(2)}) copy-start(f32[160,160]{0,1:T(8,128)S(1)} %fusion.167) | copy-start | bytes 307204
  55.5 101.3 %copy-start.10 = (f32[320,320]{0,1:T(8,128)}, f32[320,320]{0,1:T(8,128)S(1)}, u32[]{:S(2)}) copy-start(f32[320,320]{0,1:T(8,128)S(1)} %fusion.76) | copy-start | bytes 1228804
  129.3 10.6 %copy-start.4 = (f32[2,8,320,160]{2,3,1,0:T(8,128)S(1)}, f32[2,8,320,160]{2,3,1,0:T(8,128)}, u32[]{:S(2)}) copy-start(f32[2,8,320,160]{2,3,1,0:T(8,128)} %copy.146) | copy-start | bytes 9830404
  193.4 7.3 %copy-start.17 = (s32[64]{0:T(128)S(1)}, s32[64]{0:T(128)}, u32[]{:S(2)}) copy-start(s32[64]{0:T(128)} %param.13) | copy-start | bytes 772
  193.4 82.4 %all-to-all-start.1 = ((f32[2,1,8,320,160]{4,2,0,1,3:T(8,128)}), f32[2,1,8,320,160]{4,2,0,1,3:T(8,128)}, u32[]{:S(2)}, u32[]{:S(2)}) async-start(f32[2,1,8,320,160]{4,2,0,1,3:T(8,128)} %copy.158), calls=%async_computation.1 | async-start | bytes 10485760 | tf_op jit(solution)/shard_map/all_to_all | solution.py:52
  200.4 166.3 %all-reduce.2.cloned.1.call-start = ((), (), s32[]{:S(2)}) async-start(), calls=%async_computation.4 | async-start | bytes 5242880 | tf_op jit(solution)/shard_map/psum | solution.py:73
  285.6 14.0 %slice-start = ((s8[5242880]{0:T(1024)(128)(4,1)}), s8[1048576]{0:T(1024)(128)(4,1)S(1)}, s32[]{:S(2)}) async-start(s8[5242880]{0:T(1024)(128)(4,1)} %bitcast.181), calls=%async_computation.5 | async-start | bytes 2097152
  292.9 6.8 %slice-start.1 = ((s8[5242880]{0:T(1024)(128)(4,1)}), s8[4194304]{0:T(1024)(128)(4,1)S(1)}, s32[]{:S(2)}) async-start(s8[5242880]{0:T(1024)(128)(4,1)} %bitcast.181), calls=%async_computation.6 | async-start | bytes 8388608
  368.8 4.6 copy-start.5
  471.0 10.6 %copy-start.3 = (f32[2,8,320,160]{2,3,1,0:T(8,128)S(1)}, f32[2,8,320,160]{2,3,1,0:T(8,128)}, u32[]{:S(2)}) copy-start(f32[2,8,320,160]{2,3,1,0:T(8,128)} %copy.167) | copy-start | bytes 9830404
  471.0 10.6 %copy-start.7 = (f32[320,320]{0,1:T(8,128)S(1)}, f32[320,320]{0,1:T(8,128)}, u32[]{:S(2)}) copy-start(f32[320,320]{0,1:T(8,128)} %copy-done.6) | copy-start | bytes 1228804
  481.6 8.6 %copy-start.9 = (f32[320,320]{0,1:T(8,128)S(1)}, f32[320,320]{0,1:T(8,128)}, u32[]{:S(2)}) copy-start(f32[320,320]{0,1:T(8,128)} %copy-done.8) | copy-start | bytes 1228804
  490.2 8.4 %copy-start.11 = (f32[320,320]{0,1:T(8,128)S(1)}, f32[320,320]{0,1:T(8,128)}, u32[]{:S(2)}) copy-start(f32[320,320]{0,1:T(8,128)} %copy-done.10) | copy-start | bytes 1228804
  507.3 4.0 copy-start.13
  511.3 4.1 copy-start.15
  535.1 95.6 %all-to-all-start.3 = ((f32[2,1,8,320,160]{4,2,0,1,3:T(8,128)}), f32[2,1,8,320,160]{4,2,0,1,3:T(8,128)}, u32[]{:S(2)}, u32[]{:S(2)}) async-start(f32[2,1,8,320,160]{4,2,0,1,3:T(8,128)} %copy.179), calls=%async_computation.3 | async-start | bytes 10485760 | tf_op jit(solution)/shard_map/all_to_all | solution.py:52
  640.5 7.3 %copy-start.2 = (f32[2,64,20,160]{3,1,2,0:T(8,128)S(1)}, f32[2,64,20,160]{3,1,2,0:T(8,128)}, u32[]{:S(2)}) copy-start(f32[2,64,20,160]{3,1,2,0:T(8,128)} %param.9) | copy-start | bytes 4915204
  647.8 7.0 %copy-start.1 = (f32[64,64]{1,0:T(8,128)S(1)}, f32[64,64]{1,0:T(8,128)}, u32[]{:S(2)}) copy-start(f32[64,64]{1,0:T(8,128)} %param.11) | copy-start | bytes 49156
Sparse Core Ops, SparseCore 0:
  302.4 64.3 all-reduce.1
where the time goes:
time: 668 us; the launch traced here: 662 us
  waiting for transfers between devices  283 us (42%)
  matrix products  136 us (20%)
  local copies, waits for them, and re-layouts  101 us (15%)
  blocking collectives  66.3 us (10%)
  other arithmetic  32.1 us (5%)
  starting transfers between devices  23 us (3%)
  between operations  20.5 us (3%)
    all_to_all x2, waiting for transfers between devices, regroup_apply(): lax.all_to_all(smooth, 'tile', split_axis=3, concat_axis=1, tiled=True)  160 us
    dot_general x8, matrix products, horizontal(): stepped = jnp.einsum('ij,...jy->...iy', along_x, fields, precision=highest)  72.2 us
    all_to_all x1, blocking collectives, regroup_apply(): lax.all_to_all(packed, 'tile', split_axis=1, concat_axis=3, tiled=True)  66.3 us
    psum x1, waiting for transfers between devices, shards(): wind_full = lax.psum(partial_wind, 'mem') * member_scale  64.5 us
    all_to_all x1, waiting for transfers between devices, regroup_apply(): lax.all_to_all(packed, 'tile', split_axis=1, concat_axis=3, tiled=True)  58.6 us
    dot_general x8, matrix products, horizontal(): stepped = jnp.einsum('...iy,ly->...il', stepped, along_y, precision=highest)  43 us
    gather x2, local copies, waits for them, and re-layouts, regroup_apply(): packed = jnp.take(data_in, slot_level.reshape(-1), axis=1)  23.2 us
    all_to_all x2, starting transfers between devices, regroup_apply(): lax.all_to_all(smooth, 'tile', split_axis=3, concat_axis=1, tiled=True)  15.7 us
  transfers between devices with their start and end apart: 4, of which 4 were waited for; matrix products, arithmetic and copies ran while one was open for 3% of the time, Pallas kernels for 0%

commit v1 on v0

v1 whole, which is shorter than its diff:
```python
import math

import jax
import jax.numpy as jnp
import ml_dtypes
import numpy as np
from jax import lax
from jax.experimental import pallas as pl
from jax.experimental.pallas import tpu as pltpu
from jax.sharding import PartitionSpec as P

DILATIONS = (1, 2, 4, 8)
TILES = 16
MEMS = 8
ROWS = 20
NX = 320
NY = 160
LV = 64
MAIN = 128
TAIL = 32
GROUPS = ROWS // 4
K = ROWS + GROUPS
STEP = 5
FIELDS = 8
NS = len(DILATIONS)
YC = NS * NY
VMEM = 56 * 1024 * 1024
bf16 = jnp.bfloat16
f32 = jnp.float32


def line_filter(length, dilation):
    positions = np.arange(length)
    distance = np.abs(positions[None, :] - positions[:, None])
    inside = (distance % dilation == 0) & (distance <= 6 * dilation)
    ratio = (distance // dilation).astype(np.float64)
    kernel = np.where(inside, np.exp(-ratio * ratio / 8.0), 0.0)
    cubed = kernel @ kernel @ kernel
    centre = cubed[:, length // 2]
    return cubed / np.sqrt(np.sum(centre * centre))


def split_np(a):
    hi = a.astype(np.float32).astype(ml_dtypes.bfloat16)
    lo = (a - hi.astype(np.float64)).astype(np.float32).astype(ml_dtypes.bfloat16)
    return hi, lo


def x_order():
    order = []
    for j in range(4):
        for g in range(GROUPS):
            for t in range(TILES):
                order.append(ROWS * t + 4 * g + j)
    return np.array(order)


def constants():
    order = x_order()
    gx = np.concatenate(
        [line_filter(NX, d)[order][:, order] for d in DILATIONS], axis=1
    )
    gys = [line_filter(NY, d).T for d in DILATIONS]
    gy = np.concatenate([g[:, :MAIN] for g in gys] + [g[:, MAIN:] for g in gys], axis=1)
    return split_np(gx), split_np(gy)


def split(a):
    hi = a.astype(bf16)
    lo = (a - hi.astype(f32)).astype(bf16)
    return hi, lo


def dot(a, b):
    return jnp.dot(a, b, preferred_element_type=f32)


def params():
    return pltpu.CompilerParams(vmem_limit_bytes=VMEM)


def pack_body(x_ref, o_ref):
    for r in range(ROWS):
        o_ref[0, :, r] = x_ref[0, r, :, :MAIN].reshape(LV // 8, 8, MAIN)
    for g in range(GROUPS):
        tails = [x_ref[0, 4 * g + j, :, MAIN:] for j in range(4)]
        o_ref[0, :, ROWS + g] = jnp.concatenate(tails, axis=1).reshape(LV // 8, 8, MAIN)


def pack(x):
    n = x.shape[0]
    return pl.pallas_call(
        pack_body,
        grid=(n,),
        in_specs=[pl.BlockSpec((1, ROWS, LV, NY), lambda i: (i, 0, 0, 0))],
        out_specs=pl.BlockSpec((1, LV // 8, K, 8, MAIN), lambda i: (i, 0, 0, 0, 0)),
        out_shape=jax.ShapeDtypeStruct((n, LV // 8, K, 8, MAIN), f32),
        compiler_params=params(),
        name="pack",
    )(x)


def finish_body(y_ref, c_ref, o_ref):
    for r in range(ROWS):
        o_ref[0, r, :, :MAIN] = c_ref[0, r, :, :MAIN] + y_ref[0, :, r].reshape(LV, MAIN)
    for g in range(GROUPS):
        tails = y_ref[0, :, ROWS + g].reshape(LV, MAIN)
        for j in range(4):
            r = 4 * g + j
            o_ref[0, r, :, MAIN:] = c_ref[0, r, :, MAIN:] + tails[:, TAIL * j : TAIL * (j + 1)]


def finish(y, control):
    n = y.shape[0]
    natural = pl.BlockSpec((1, ROWS, LV, NY), lambda i: (i, 0, 0, 0))
    return pl.pallas_call(
        finish_body,
        grid=(n,),
        in_specs=[pl.BlockSpec((1, LV // 8, K, 8, MAIN), lambda i: (i, 0, 0, 0, 0)), natural],
        out_specs=natural,
        out_shape=jax.ShapeDtypeStruct((n, ROWS, LV, NY), f32),
        compiler_params=params(),
        name="finish",
    )(y, control)


def field_rows(k, f):
    return pl.ds(8 * k + f, TILES, stride=8 * K)


def filter_body(x_ref, w_ref, gy_ref, gxs_ref, gxh_ref, o_ref, hi_ref, lo_ref):
    for j in range(4):
        parts = []
        for f in range(FIELDS):
            for g in range(GROUPS):
                pair = [x_ref[field_rows(k, f), :] for k in (4 * g + j, ROWS + g)]
                parts.append(jnp.concatenate(pair, axis=1))
        hi, lo = split(jnp.concatenate(parts, axis=0))
        y = dot(jnp.concatenate([hi, lo, hi], axis=1), gy_ref[j])
        span = TILES * GROUPS
        fields = [y[span * f : span * (f + 1)] * w_ref[f : f + 1, :] for f in range(FIELDS)]
        for s in range(NS):
            at = s * NX + j * span
            pieces = [fields[f][:, MAIN * s : MAIN * (s + 1)] for f in range(FIELDS)]
            for q in range(FIELDS // 4):
                lane = NS * MAIN + TAIL * s
                pieces.append(
                    jnp.concatenate(
                        [fields[4 * q + i][:, lane : lane + TAIL] for i in range(4)], axis=1
                    )
                )
            hi, lo = split(jnp.concatenate(pieces, axis=1))
            hi_ref[at : at + span, :] = hi
            lo_ref[at : at + span, :] = lo
    both = dot(gxs_ref[...], hi_ref[...])
    out = both[:NX] + both[NX:] + dot(gxh_ref[...], lo_ref[...])
    for f in range(FIELDS):
        for g in range(GROUPS):
            tails = []
            lane = FIELDS * MAIN + MAIN * (f // 4) + TAIL * (f % 4)
            for j in range(4):
                at = TILES * (GROUPS * j + g)
                o_ref[field_rows(4 * g + j, f), :] = out[
                    at : at + TILES, MAIN * f : MAIN * (f + 1)
                ]
                tails.append(out[at : at + TILES, lane : lane + TAIL])
            o_ref[field_rows(ROWS + g, f), :] = jnp.concatenate(tails, axis=1)


def filter_fields(x, w, gy, gxs, gxh):
    return pl.pallas_call(
        filter_body,
        out_shape=jax.ShapeDtypeStruct((TILES * K * FIELDS, MAIN), f32),
        scratch_shapes=[
            pltpu.VMEM((NS * NX, FIELDS * NY), bf16),
            pltpu.VMEM((NS * NX, FIELDS * NY), bf16),
        ],
        compiler_params=params(),
        name="filter",
    )(x, w, gy, gxs, gxh)


def mix(v_ref, x):
    hi, lo = split(x)
    vh, vl = split(v_ref[...])
    return dot(vh, hi) + dot(vh, lo) + dot(vl, hi)


def levels_at(ref, lead, at):
    tiles = [ref[lead + (slice(None), at + i)].reshape(LV, MAIN) for i in range(STEP)]
    return jnp.concatenate(tiles, axis=1)


def forward_body(x_ref, v_ref, e_ref, o_ref):
    for at in range(0, K, STEP):
        loc = [mix(v_ref, levels_at(x_ref, (m,), at)) for m in range(2)]
        for c in range(2):
            total = sum(levels_at(e_ref, (m, c), at) * loc[m] for m in range(2))
            for i in range(STEP):
                o_ref[:, c, at + i] = total[:, MAIN * i : MAIN * (i + 1)].reshape(MEMS, 8, MAIN)


def forward(x, v, ens):
    return pl.pallas_call(
        forward_body,
        out_shape=jax.ShapeDtypeStruct((MEMS, 2, K, 8, MAIN), f32),
        compiler_params=params(),
        name="forward",
    )(x, v, ens)


def total_body(scale, x_ref, o_ref, wind_ref):
    for c in range(2):
        total = x_ref[0, c]
        for k in range(1, MEMS):
            total = total + x_ref[k, c]
        total = total * scale
        for k in range(MEMS):
            o_ref[k, c] = total
        for r in range(ROWS):
            wind_ref[c, r, :, :MAIN] = total[r]
        for g in range(GROUPS):
            for j in range(4):
                wind_ref[c, 4 * g + j, :, MAIN:] = total[ROWS + g][:, TAIL * j : TAIL * (j + 1)]


def total(x, scale):
    return pl.pallas_call(
        lambda *refs: total_body(scale, *refs),
        out_shape=(
            jax.ShapeDtypeStruct((MEMS, 2, K, 8, MAIN), f32),
            jax.ShapeDtypeStruct((2, ROWS, LV // MEMS, NY), f32),
        ),
        compiler_params=params(),
        name="total",
    )(x)


def adjoint_body(scale, x_ref, v_ref, e_ref, o_ref):
    for at in range(0, K, STEP):
        wind = []
        for c in range(2):
            tiles = [x_ref[:, c, at + i].reshape(LV, MAIN) for i in range(STEP)]
            wind.append(jnp.concatenate(tiles, axis=1))
        for m in range(2):
            adj = sum(levels_at(e_ref, (m, c), at) * wind[c] for c in range(2)) * scale
            back = mix(v_ref, adj)
            for i in range(STEP):
                o_ref[m, :, at + i] = back[:, MAIN * i : MAIN * (i + 1)].reshape(LV // 8, 8, MAIN)


def adjoint(x, v, ens, scale):
    return pl.pallas_call(
        lambda *refs: adjoint_body(scale, *refs),
        out_shape=jax.ShapeDtypeStruct((2, LV // 8, K, 8, MAIN), f32),
        compiler_params=params(),
        name="adjoint",
    )(x, v, ens)


def tiles_swap(x):
    return lax.all_to_all(x.reshape(TILES, K, FIELDS, MAIN), "tile", 0, 0, tiled=True)


def shards(control, ens_perts, vert_corr, slab_wts, level_slab):
    members = control.shape[0]
    scale = 1.0 / math.sqrt(members * MEMS - 1)
    (gxh, gxl), (gyh, gyl) = constants()

    control = jnp.transpose(control, (0, 2, 1, 3))
    ens = jnp.transpose(ens_perts, (0, 1, 3, 2, 4)).reshape(4, ROWS, LV, NY)
    sent = pack(control)
    got = tiles_swap(sent)

    ens = pack(ens).reshape(2, 2, LV // 8, K, 8, MAIN)
    gxs = jnp.concatenate([jnp.asarray(gxh), jnp.asarray(gxl)], axis=0)
    variants = []
    for j in range(4):
        def wide(g):
            zeros = jnp.zeros((MAIN, YC), bf16)
            return jnp.concatenate([jnp.asarray(g[:MAIN]), zeros.at[TAIL * j : TAIL * (j + 1)].set(jnp.asarray(g[MAIN:]))], axis=0)
        high = wide(gyh)
        variants.append(jnp.concatenate([high, high, wide(gyl)], axis=0))
    gy = jnp.stack(variants)
    level_wts = slab_wts[level_slab]
    first = FIELDS * (lax.axis_index("tile") % (LV // FIELDS))
    own = lax.dynamic_slice_in_dim(level_wts, first, FIELDS, 0)
    w = jnp.concatenate([jnp.repeat(own, MAIN, axis=1), jnp.repeat(own, TAIL, axis=1)], axis=1)

    def smooth(x):
        return filter_fields(x.reshape(TILES * K * FIELDS, MAIN), w, gy, gxs, jnp.asarray(gxh))

    back = tiles_swap(smooth(got)).reshape(2, LV // 8, K, 8, MAIN)
    part = forward(back, vert_corr, ens)
    pieces = lax.all_to_all(part, "mem", 0, 0, tiled=True)
    copies, wind_share = total(pieces, scale)
    wind = lax.all_to_all(copies, "mem", 0, 0, tiled=True)
    adj = adjoint(wind, vert_corr.T, ens, scale)
    back = tiles_swap(smooth(tiles_swap(adj))).reshape(2, LV // 8, K, 8, MAIN)
    gradient = finish(back, control)
    return (jnp.transpose(wind_share, (0, 2, 1, 3)), jnp.transpose(gradient, (0, 2, 1, 3)))


def solution(mesh):
    return jax.shard_map(
        shards,
        mesh=mesh,
        in_specs=(P("mem", None, "tile", None), P("mem", None, None, "tile", None), P(), P(), P()),
        out_specs=(P(None, "mem", "tile", None), P("mem", None, "tile", None)),
        check_vma=False,
    )
```

time: 668 us -> 213 us (0.32)
  the two profiles are of different devices: /device:TPU:116 before, /device:TPU:0 now
where the time goes in v1:
time: 213 us
  blocking collectives  81.5 us (38%)
  waiting for transfers between devices  62 us (29%)
  Pallas kernels  46.7 us (22%)
  starting transfers between devices  15.9 us (7%)
  local copies, waits for them, and re-layouts  5.2 us (2%)
    all_to_all x2, blocking collectives, tiles_swap(): lax.all_to_all(x.reshape(TILES, K, FIELDS, MAIN), 'tile', 0, 0, tiled=True)  54.8 us
    all_to_all x2, waiting for transfers between devices, tiles_swap(): lax.all_to_all(x.reshape(TILES, K, FIELDS, MAIN), 'tile', 0, 0, tiled=True)  40.5 us
    all_to_all x1, blocking collectives, shards(): pieces = lax.all_to_all(part, 'mem', 0, 0, tiled=True)  26.7 us
    pallas_call x2, Pallas kernels, filter_fields(): pl.pallas_call(filter_body, out_shape=jax.ShapeDtypeStruct((TILES * K * F...  23.7 us
    all_to_all x1, waiting for transfers between devices, shards(): wind = lax.all_to_all(copies, 'mem', 0, 0, tiled=True)  21.5 us
    all_to_all x2, starting transfers between devices, tiles_swap(): lax.all_to_all(x.reshape(TILES, K, FIELDS, MAIN), 'tile', 0, 0, tiled=True)  12.2 us
    pallas_call x2, Pallas kernels, pack(): pl.pallas_call(pack_body, grid=(n,), in_specs=[pl.BlockSpec((1, ROWS, LV,...  7.8 us
    pallas_call x1, Pallas kernels, adjoint(): pl.pallas_call(lambda *refs: adjoint_body(scale, *refs), out_shape=jax.Sh...  4.47 us
  transfers between devices with their start and end apart: 3, of which 3 were waited for; matrix products, arithmetic and copies ran while one was open for 1% of the time, Pallas kernels for 2%

profile of v1, /device:TPU:0, one launch (start us, length us, event | category | flops | bytes accessed | tf_op | source)
XLA Modules:
  0.0 212.6 jit_solution(7805955262747016786)
XLA Ops:
  0.6 2.8 %pack.2 = f32[2,8,25,8,128]{4,3,2,1,0:T(8,128)} custom-call(f32[2,20,64,160]{3,2,1,0:T(8,128)} %bitcast.20), custom_call_target="tpu_custom_call" | custom-call | tf_op jit(solution)/shard_map/pack/pallas_call | solution.py:92
  3.4 0.0 copy-start.4
  3.4 8.3 %all-to-all-start = ((f32[16,25,8,128]{3,2,1,0:T(8,128)}), f32[16,25,8,128]{3,2,1,0:T(8,128)S(1)}, u32[]{:S(2)}, u32[]{:S(2)}) async-start(f32[16,25,8,128]{3,2,1,0:T(8,128)} %bitcast.22), calls=%async_computation | async-start | bytes 3276800 | tf_op jit(solution)/shard_map/all_to_all | solution.py:262
  11.8 0.0 copy-done.4
  11.8 0.1 copy.25
  11.8 0.0 copy-done.5
  11.9 0.6 gather_fusion
  12.5 0.1 copy.26
  12.6 0.1 broadcast_in_dim.11
  12.6 0.1 reshape.230
  12.7 0.1 broadcast_bitcast_fusion
  12.8 0.6 pad_maximum_fusion.w_ref
  13.4 22.9 %all-to-all-done = f32[16,25,8,128]{3,2,1,0:T(8,128)S(1)} async-done(((f32[16,25,8,128]{3,2,1,0:T(8,128)}), f32[16,25,8,128]{3,2,1,0:T(8,128)S(1)}, u32[]{:S(2)}, u32[]{:S(2)}) %all-to-all-start) | async-done | bytes 1638432 | tf_op jit(solution)/shard_map/all_to_all | solution.py:262
  36.3 1.2 copy-done.2
  37.5 11.9 %filter.2 = f32[3200,128]{1,0:T(8,128)} custom-call(f32[3200,128]{1,0:T(8,128)} %bitcast.25, f32[8,640]{1,0:T(8,128)} %pad_maximum_fusion.w_ref, bf16[4,768,640]{2,1,0:T(8,128)(2,1)} %constant.260.gy_ref, bf16[640,1280]{1,0:T(8,128)(2,1)} %constant.261.gxs_ref, bf16[320,1280]{1,0:T(8,128)(2,1)} %constant.220.clone.gxh_ref), custom_call_target="tpu_custom_call" | custom-call | tf_op jit(solution)/shard_map/filter/pallas_call | solution.py:171
  49.4 3.9 %all-to-all-start.1 = ((f32[16,25,8,128]{3,2,1,0:T(8,128)}), f32[16,25,8,128]{3,2,1,0:T(8,128)S(1)}, u32[]{:S(2)}, u32[]{:S(2)}) async-start(f32[16,25,8,128]{3,2,1,0:T(8,128)} %bitcast.26), calls=%async_computation.1 | async-start | bytes 3276800 | tf_op jit(solution)/shard_map/all_to_all | solution.py:262
  53.2 5.0 %pack.3 = f32[4,8,25,8,128]{4,3,2,1,0:T(8,128)} custom-call(f32[4,20,64,160]{3,2,1,0:T(8,128)} %bitcast.30), custom_call_target="tpu_custom_call" | custom-call | tf_op jit(solution)/shard_map/pack/pallas_call | solution.py:92
  58.2 17.6 %all-to-all-done.1 = f32[16,25,8,128]{3,2,1,0:T(8,128)S(1)} async-done(((f32[16,25,8,128]{3,2,1,0:T(8,128)}), f32[16,25,8,128]{3,2,1,0:T(8,128)S(1)}, u32[]{:S(2)}, u32[]{:S(2)}) %all-to-all-start.1) | async-done | bytes 1638432 | tf_op jit(solution)/shard_map/all_to_all | solution.py:262
  75.8 1.2 copy-done.1
  77.0 4.4 %forward.1 = f32[8,2,25,8,128]{4,3,2,1,0:T(8,128)} custom-call(f32[2,8,25,8,128]{4,3,2,1,0:T(8,128)} %bitcast.23, f32[64,64]{1,0:T(8,128)} %v_ref.1, f32[2,2,8,25,8,128]{5,4,3,2,1,0:T(8,128)} %bitcast.18), custom_call_target="tpu_custom_call" | custom-call | tf_op jit(solution)/shard_map/forward/pallas_call | solution.py:204
  81.4 26.7 %all_to_all.30.refs_0_ = f32[8,2,25,8,128]{4,3,2,1,0:T(8,128)} all-to-all(f32[8,2,25,8,128]{4,3,2,1,0:T(8,128)} %forward.1), channel_id=1, replica_groups=mesh['mem'=8,'tile'=16] {'mem'}, dimensions={0} | all-to-all | bytes 3276800 | tf_op jit(solution)/shard_map/all_to_all | solution.py:295
  108.1 2.8 %total.1 = (f32[8,2,25,8,128]{4,3,2,1,0:T(8,128)}, f32[2,20,8,160]{3,2,1,0:T(8,128)}) custom-call(f32[8,2,25,8,128]{4,3,2,1,0:T(8,128)} %all_to_all.30.refs_0_), custom_call_target="tpu_custom_call" | custom-call | tf_op jit(solution)/shard_map/total/pallas_call | solution.py:228
  110.9 3.7 %all-to-all-start.3 = ((f32[8,2,25,8,128]{4,3,2,1,0:T(8,128)}), f32[8,2,25,8,128]{4,3,2,1,0:T(8,128)S(1)}, u32[]{:S(2)}, u32[]{:S(2)}) async-start(f32[8,2,25,8,128]{4,3,2,1,0:T(8,128)} %get-tuple-element.101), calls=%async_computation.3 | async-start | bytes 3276800 | tf_op jit(solution)/shard_map/all_to_all | solution.py:297
  114.7 0.0 copy-done.3
  114.7 0.7 copy.27
  115.4 21.5 %all-to-all-done.3.refs_0_ = f32[8,2,25,8,128]{4,3,2,1,0:T(8,128)S(1)} async-done(((f32[8,2,25,8,128]{4,3,2,1,0:T(8,128)}), f32[8,2,25,8,128]{4,3,2,1,0:T(8,128)S(1)}, u32[]{:S(2)}, u32[]{:S(2)}) %all-to-all-start.3) | async-done | bytes 1638432 | tf_op jit(solution)/shard_map/all_to_all | solution.py:297
  136.9 1.2 copy-done
  138.0 4.5 %adjoint.1 = f32[2,8,25,8,128]{4,3,2,1,0:T(8,128)} custom-call(f32[8,2,25,8,128]{4,3,2,1,0:T(8,128)} %copy-done, f32[64,64]{1,0:T(8,128)} %bitcast.32, f32[2,2,8,25,8,128]{5,4,3,2,1,0:T(8,128)} %bitcast.19), custom_call_target="tpu_custom_call" | custom-call | tf_op jit(solution)/shard_map/adjoint/pallas_call | solution.py:253
  142.5 28.0 %all_to_all.31 = f32[16,25,8,128]{3,2,1,0:T(8,128)} all-to-all(f32[16,25,8,128]{3,2,1,0:T(8,128)} %bitcast.24), channel_id=1, replica_groups=mesh['mem'=8,'tile'=16] {'tile'}, dimensions={0} | all-to-all | bytes 3276800 | tf_op jit(solution)/shard_map/all_to_all | solution.py:262
  170.5 11.8 %filter.3 = f32[3200,128]{1,0:T(8,128)} custom-call(f32[3200,128]{1,0:T(8,128)} %bitcast.27, f32[8,640]{1,0:T(8,128)} %pad_maximum_fusion.w_ref, bf16[4,768,640]{2,1,0:T(8,128)(2,1)} %constant.260.gy_ref, bf16[640,1280]{1,0:T(8,128)(2,1)} %constant.261.gxs_ref, bf16[320,1280]{1,0:T(8,128)(2,1)} %constant.220.clone.gxh_ref), custom_call_target="tpu_custom_call" | custom-call | tf_op jit(solution)/shard_map/filter/pallas_call | solution.py:171
  182.3 26.8 %all_to_all.32 = f32[16,25,8,128]{3,2,1,0:T(8,128)} all-to-all(f32[16,25,8,128]{3,2,1,0:T(8,128)} %bitcast.28), channel_id=1, replica_groups=mesh['mem'=8,'tile'=16] {'tile'}, dimensions={0} | all-to-all | bytes 3276800 | tf_op jit(solution)/shard_map/all_to_all | solution.py:262
  209.1 3.5 %finish.1 = f32[2,20,64,160]{3,2,1,0:T(8,128)} custom-call(f32[2,8,25,8,128]{4,3,2,1,0:T(8,128)} %bitcast.29, f32[2,20,64,160]{3,2,1,0:T(8,128)} %bitcast.21), custom_call_target="tpu_custom_call" | custom-call | tf_op jit(solution)/shard_map/finish/pallas_call | solution.py:116
  (8 shorter events, 0.0 us)
Async XLA Ops:
  3.4 8.3 %copy-start.4 = (f32[16,4]{0,1:T(4,128)S(1)}, f32[16,4]{0,1:T(4,128)}, u32[]{:S(2)}) copy-start(f32[16,4]{0,1:T(4,128)} %param.42) | copy-start | bytes 772
  3.4 8.4 %copy-start.5 = (s32[64]{0:T(128)S(1)}, s32[64]{0:T(128)}, u32[]{:S(2)}) copy-start(s32[64]{0:T(128)} %param.43) | copy-start | bytes 772
  3.4 32.9 %all-to-all-start = ((f32[16,25,8,128]{3,2,1,0:T(8,128)}), f32[16,25,8,128]{3,2,1,0:T(8,128)S(1)}, u32[]{:S(2)}, u32[]{:S(2)}) async-start(f32[16,25,8,128]{3,2,1,0:T(8,128)} %bitcast.22), calls=%async_computation | async-start | bytes 3276800 | tf_op jit(solution)/shard_map/all_to_all | solution.py:262
  36.3 1.2 copy-start.2
  49.4 26.4 %all-to-all-start.1 = ((f32[16,25,8,128]{3,2,1,0:T(8,128)}), f32[16,25,8,128]{3,2,1,0:T(8,128)S(1)}, u32[]{:S(2)}, u32[]{:S(2)}) async-start(f32[16,25,8,128]{3,2,1,0:T(8,128)} %bitcast.26), calls=%async_computation.1 | async-start | bytes 3276800 | tf_op jit(solution)/shard_map/all_to_all | solution.py:262
  75.8 1.2 copy-start.1
  110.9 3.7 %copy-start.3 = (f32[64,64]{1,0:T(8,128)S(1)}, f32[64,64]{1,0:T(8,128)}, u32[]{:S(2)}) copy-start(f32[64,64]{1,0:T(8,128)} %v_ref.1) | copy-start | bytes 49156
  110.9 25.9 %all-to-all-start.3 = ((f32[8,2,25,8,128]{4,3,2,1,0:T(8,128)}), f32[8,2,25,8,128]{4,3,2,1,0:T(8,128)S(1)}, u32[]{:S(2)}, u32[]{:S(2)}) async-start(f32[8,2,25,8,128]{4,3,2,1,0:T(8,128)} %get-tuple-element.101), calls=%async_computation.3 | async-start | bytes 3276800 | tf_op jit(solution)/shard_map/all_to_all | solution.py:297
  136.8 1.2 copy-start

commit v2 on v1

v2 whole, which is shorter than its diff:
```python
import math

import jax
import jax.numpy as jnp
import ml_dtypes
import numpy as np
from jax import lax
from jax.experimental import pallas as pl
from jax.experimental.pallas import tpu as pltpu
from jax.sharding import PartitionSpec as P


DILATIONS = (1, 2, 4, 8)
TILES = 16
MEMS = 8
ROWS = 20
NX = 320
NY = 160
LV = 64
MAIN = 128
TAIL = 32
GROUPS = ROWS // 4
K = ROWS + GROUPS
Q = 4
FIELDS = 8
NS = len(DILATIONS)
VMEM = 56 * 1024 * 1024
bf16 = jnp.bfloat16
f32 = jnp.float32


def line_filter(length, dilation):
    positions = np.arange(length)
    distance = np.abs(positions[None, :] - positions[:, None])
    inside = (distance % dilation == 0) & (distance <= 6 * dilation)
    ratio = (distance // dilation).astype(np.float64)
    kernel = np.where(inside, np.exp(-ratio * ratio / 8.0), 0.0)
    cubed = kernel @ kernel @ kernel
    centre = cubed[:, length // 2]
    return cubed / np.sqrt(np.sum(centre * centre))


def split_np(a):
    hi = a.astype(np.float32).astype(ml_dtypes.bfloat16)
    lo = (a - hi.astype(np.float64)).astype(np.float32).astype(ml_dtypes.bfloat16)
    return hi, lo


def x_order():
    order = []
    for j in range(4):
        for g in range(GROUPS):
            for t in range(TILES):
                order.append(ROWS * t + 4 * g + j)
    return np.array(order)


def constants():
    order = x_order()
    gx = np.concatenate(
        [line_filter(NX, d)[order][:, order] for d in DILATIONS], axis=1
    )
    gys = [line_filter(NY, d).T for d in DILATIONS]
    gy = np.concatenate([g[:, :MAIN] for g in gys] + [g[:, MAIN:] for g in gys], axis=1)
    gy = np.concatenate([gy, np.zeros((2 * MAIN - NY, NS * NY))], axis=0)
    return split_np(gx), split_np(gy)


def split(a):
    hi = a.astype(bf16)
    lo = (a - hi.astype(f32)).astype(bf16)
    return hi, lo


def dot(a, b):
    return jnp.dot(a, b, preferred_element_type=f32)


def params():
    return pltpu.CompilerParams(vmem_limit_bytes=VMEM)


def pack_body(x_ref, o_ref):
    for r in range(ROWS):
        o_ref[0, :, r] = x_ref[0, r, :, :MAIN].reshape(LV // 8, 8, MAIN)
    for g in range(GROUPS):
        tails = [x_ref[0, 4 * g + j, :, MAIN:] for j in range(4)]
        o_ref[0, :, ROWS + g] = jnp.concatenate(tails, axis=1).reshape(LV // 8, 8, MAIN)


def pack(x):
    n = x.shape[0]
    return pl.pallas_call(
        pack_body,
        grid=(n,),
        in_specs=[pl.BlockSpec((1, ROWS, LV, NY), lambda i: (i, 0, 0, 0))],
        out_specs=pl.BlockSpec((1, LV // 8, K, 8, MAIN), lambda i: (i, 0, 0, 0, 0)),
        out_shape=jax.ShapeDtypeStruct((n, LV // 8, K, 8, MAIN), f32),
        compiler_params=params(),
        name="pack",
    )(x)


def finish_body(y_ref, c_ref, o_ref):
    for r in range(ROWS):
        o_ref[0, r, :, :MAIN] = c_ref[0, r, :, :MAIN] + y_ref[0, :, r].reshape(LV, MAIN)
    for g in range(GROUPS):
        tails = y_ref[0, :, ROWS + g].reshape(LV, MAIN)
        for j in range(4):
            r = 4 * g + j
            o_ref[0, r, :, MAIN:] = c_ref[0, r, :, MAIN:] + tails[:, TAIL * j : TAIL * (j + 1)]


def finish(y, control):
    n = y.shape[0]
    natural = pl.BlockSpec((1, ROWS, LV, NY), lambda i: (i, 0, 0, 0))
    return pl.pallas_call(
        finish_body,
        grid=(n,),
        in_specs=[pl.BlockSpec((1, LV // 8, K, 8, MAIN), lambda i: (i, 0, 0, 0, 0)), natural],
        out_specs=natural,
        out_shape=jax.ShapeDtypeStruct((n, ROWS, LV, NY), f32),
        compiler_params=params(),
        name="finish",
    )(y, control)


def unpack_wind_body(x_ref, o_ref):
    for c in range(2):
        for r in range(ROWS):
            o_ref[c, r, :, :MAIN] = x_ref[r % MEMS, c, r // MEMS]
        for g in range(GROUPS):
            k = ROWS + g
            tails = x_ref[k % MEMS, c, k // MEMS]
            for j in range(4):
                o_ref[c, 4 * g + j, :, MAIN:] = tails[:, TAIL * j : TAIL * (j + 1)]


def unpack_wind(x):
    return pl.pallas_call(
        unpack_wind_body,
        out_shape=jax.ShapeDtypeStruct((2, ROWS, LV // MEMS, NY), f32),
        compiler_params=params(),
        name="unpack_wind",
    )(x)


def spread_body(me_ref, x_ref, *refs):
    o_refs, packed = refs[:MEMS], refs[MEMS]
    for r in range(ROWS):
        packed[r % MEMS, r // MEMS] = x_ref[0, r, :, :MAIN]
    for g in range(GROUPS):
        tails = [x_ref[0, 4 * g + j, :, MAIN:] for j in range(4)]
        k = ROWS + g
        packed[k % MEMS, k // MEMS] = jnp.concatenate(tails, axis=1)
    for k in range(K, MEMS * Q):
        packed[k % MEMS, k // MEMS] = jnp.zeros((LV, MAIN), f32)
    for k in range(MEMS):
        o_refs[k][0] = packed[lax.rem(me_ref[0] + k, MEMS)]


def spread(me, x):
    n = x.shape[0]
    return pl.pallas_call(
        spread_body,
        grid_spec=pltpu.PrefetchScalarGridSpec(
            num_scalar_prefetch=1,
            grid=(n,),
            in_specs=[pl.BlockSpec((1, ROWS, LV, NY), lambda i, me: (i, 0, 0, 0))],
            out_specs=[pl.BlockSpec((1, Q, LV, MAIN), lambda i, me: (i, 0, 0, 0))] * MEMS,
            scratch_shapes=[pltpu.VMEM((MEMS, Q, LV, MAIN), f32)],
        ),
        out_shape=[jax.ShapeDtypeStruct((n, Q, LV, MAIN), f32)] * MEMS,
        compiler_params=params(),
        name="spread",
    )(me, x)


def field_rows(k, f):
    return pl.ds(8 * k + f, TILES, stride=8 * K)


def share_rows(k, f):
    at = ((k % MEMS) * TILES * Q + k // MEMS) * 8 + f
    return pl.ds(at, TILES, stride=8 * Q)


def filter_body(in_rows, out_rows, x_ref, w_ref, gy_ref, gx_ref, o_ref, hi_ref, lo_ref):
    span = TILES * GROUPS
    for j in range(4):
        parts = []
        for f in range(FIELDS):
            for g in range(GROUPS):
                tail = x_ref[in_rows(ROWS + g, f), :]
                if j:
                    tail = pltpu.roll(tail, MAIN - TAIL * j, 1)
                main = x_ref[in_rows(4 * g + j, f), :]
                parts.append(jnp.concatenate([main, tail], axis=1))
        hi, lo = split(jnp.concatenate(parts, axis=0))
        y = dot(jnp.concatenate([hi, lo, hi], axis=1), gy_ref[...])
        fields = [y[span * f : span * (f + 1)] * w_ref[f : f + 1, :] for f in range(FIELDS)]
        for s in range(NS):
            at = s * NX + j * span
            pieces = [fields[f][:, MAIN * s : MAIN * (s + 1)] for f in range(FIELDS)]
            for q in range(FIELDS // 4):
                lane = NS * MAIN + TAIL * s
                pieces.append(
                    jnp.concatenate(
                        [fields[4 * q + i][:, lane : lane + TAIL] for i in range(4)], axis=1
                    )
                )
            hi, lo = split(jnp.concatenate(pieces, axis=1))
            hi_ref[at : at + span, :] = hi
            lo_ref[at : at + span, :] = lo
    both = dot(gx_ref[...], hi_ref[...])
    out = both[:NX] + both[NX:] + dot(gx_ref[:NX, :], lo_ref[...])
    for f in range(FIELDS):
        for g in range(GROUPS):
            tails = []
            lane = FIELDS * MAIN + MAIN * (f // 4) + TAIL * (f % 4)
            for j in range(4):
                at = TILES * (GROUPS * j + g)
                o_ref[out_rows(4 * g + j, f), :] = out[at : at + TILES, MAIN * f : MAIN * (f + 1)]
                tails.append(out[at : at + TILES, lane : lane + TAIL])
            o_ref[out_rows(ROWS + g, f), :] = jnp.concatenate(tails, axis=1)
    if out_rows is share_rows:
        for k in range(K, MEMS * Q):
            for f in range(FIELDS):
                o_ref[out_rows(k, f), :] = jnp.zeros((TILES, MAIN), f32)


def filter_fields(x, w, gy, gx, spread_out):
    rows = TILES * FIELDS * (MEMS * Q if spread_out else K)
    in_rows, out_rows = (field_rows, share_rows) if spread_out else (share_rows, field_rows)
    return pl.pallas_call(
        lambda *refs: filter_body(in_rows, out_rows, *refs),
        out_shape=jax.ShapeDtypeStruct((rows, MAIN), f32),
        scratch_shapes=[
            pltpu.VMEM((NS * NX, FIELDS * NY), bf16),
            pltpu.VMEM((NS * NX, FIELDS * NY), bf16),
        ],
        compiler_params=params(),
        name="filter_out" if spread_out else "filter_back",
    )(x, w, gy, gx)


def mix(v, x):
    hi, lo = split(x)
    return dot(v[0], hi) + dot(v[0], lo) + dot(v[1], hi)


def middle_body(scale, me_ref, x_ref, v_ref, vt_ref, *refs):
    e_refs, o_ref, wind_ref = refs[:MEMS], refs[MEMS], refs[MEMS + 1]
    v, vt = split(v_ref[...]), split(vt_ref[...])
    wind = [None, None]
    for k in range(MEMS):
        at = lax.rem(me_ref[0] + MEMS - k, MEMS)
        for m in range(2):
            tiles = [x_ref[at, m, :, q].reshape(LV, MAIN) for q in range(Q)]
            loc = mix(v, jnp.concatenate(tiles, axis=1))
            for c in range(2):
                ens = jnp.concatenate([e_refs[k][m, c, q] for q in range(Q)], axis=1)
                wind[c] = ens * loc if wind[c] is None else wind[c] + ens * loc
    wind = [w * scale for w in wind]
    for c in range(2):
        for q in range(Q):
            tile = wind[c][:, MAIN * q : MAIN * (q + 1)]
            wind_ref[:, c, q] = tile.reshape(MEMS, LV // MEMS, MAIN)
    for k in range(MEMS):
        at = lax.rem(me_ref[0] + MEMS - k, MEMS)
        for m in range(2):
            adj = None
            for c in range(2):
                ens = jnp.concatenate([e_refs[k][m, c, q] for q in range(Q)], axis=1)
                adj = ens * wind[c] if adj is None else adj + ens * wind[c]
            back = mix(vt, adj * scale)
            for q in range(Q):
                tile = back[:, MAIN * q : MAIN * (q + 1)]
                o_ref[at, m, :, q] = tile.reshape(LV // 8, 8, MAIN)


def middle(me, x, v, ens, scale):
    whole = pl.BlockSpec(memory_space=pltpu.VMEM)
    return pl.pallas_call(
        lambda *refs: middle_body(scale, *refs),
        in_specs=[pl.BlockSpec(memory_space=pltpu.SMEM)] + [whole] * (3 + MEMS),
        out_shape=(
            jax.ShapeDtypeStruct((MEMS, 2, LV // 8, Q, 8, MAIN), f32),
            jax.ShapeDtypeStruct((MEMS, 2, Q, LV // MEMS, MAIN), f32),
        ),
        compiler_params=params(),
        name="middle",
    )(me, x, v, v.T, *ens)


def swap(x, axes):
    return lax.all_to_all(x, axes, 0, 0, tiled=True)


def shards(control, ens_perts, vert_corr, slab_wts, level_slab):
    members = control.shape[0]
    scale = 1.0 / math.sqrt(members * MEMS - 1)
    (gxh, gxl), (gyh, gyl) = constants()

    control = jnp.transpose(control, (0, 2, 1, 3))
    got = swap(pack(control).reshape(TILES, K, FIELDS, MAIN), "tile")

    me = lax.axis_index("mem").reshape(1)
    ens = jnp.transpose(ens_perts, (0, 1, 3, 2, 4)).reshape(4, ROWS, LV, NY)
    ens = list(spread(me, ens))
    for k in range(1, MEMS):
        ens[k] = lax.ppermute(ens[k], "mem", [(i, (i + k) % MEMS) for i in range(MEMS)])
    ens = [e.reshape(2, 2, Q, LV, MAIN) for e in ens]

    gx = jnp.asarray(np.concatenate([gxh, gxl], axis=0))
    gy = jnp.asarray(np.concatenate([gyh, gyh, gyl], axis=0))
    level_wts = slab_wts[level_slab]
    first = FIELDS * (lax.axis_index("tile") % (LV // FIELDS))
    own = lax.dynamic_slice_in_dim(level_wts, first, FIELDS, 0)
    w = jnp.concatenate([jnp.repeat(own, MAIN, axis=1), jnp.repeat(own, TAIL, axis=1)], axis=1)

    smooth = filter_fields(got.reshape(TILES * K * FIELDS, MAIN), w, gy, gx, True)
    got = swap(smooth.reshape(MEMS * TILES, Q, FIELDS, MAIN), ("mem", "tile"))
    got = got.reshape(MEMS, 2, LV // 8, Q, 8, MAIN)
    adj, wind = middle(me, got, vert_corr, ens, scale)
    got = swap(adj.reshape(MEMS * TILES, Q, FIELDS, MAIN), ("mem", "tile"))
    got, wind = lax.optimization_barrier((got, wind))
    wind = unpack_wind(swap(wind, "mem"))
    smooth = filter_fields(got.reshape(MEMS * TILES * Q * FIELDS, MAIN), w, gy, gx, False)
    got = swap(smooth.reshape(TILES, K, FIELDS, MAIN), "tile")
    gradient = finish(got.reshape(2, LV // 8, K, 8, MAIN), control)
    return (jnp.transpose(wind, (0, 2, 1, 3)), jnp.transpose(gradient, (0, 2, 1, 3)))


def solution(mesh):
    return jax.shard_map(
        shards,
        mesh=mesh,
        in_specs=(P("mem", None, "tile", None), P("mem", None, None, "tile", None), P(), P(), P()),
        out_specs=(P(None, "mem", "tile", None), P("mem", None, "tile", None)),
        check_vma=False,
    )
```

time: 213 us -> 222 us (1.042)
  the two profiles are of different devices: /device:TPU:0 before, /device:TPU:2 now
where the time goes in v2:
time: 222 us
  waiting for transfers between devices  87.9 us (40%)
  Pallas kernels  43.3 us (20%)
  starting transfers between devices  43 us (19%)
  blocking collectives  40.7 us (18%)
  local copies, waits for them, and re-layouts  5.42 us (2%)
    all_to_all x4, waiting for transfers between devices, swap(): return lax.all_to_all(x, axes, 0, 0, tiled=True)  46.9 us
    ppermute x7, waiting for transfers between devices, shards(): lax.ppermute(ens[k], 'mem', [(i, (i + k) % MEMS) for i in range(MEMS)])  41 us
    all_to_all x1, blocking collectives, swap(): return lax.all_to_all(x, axes, 0, 0, tiled=True)  40.7 us
    pallas_call x2, Pallas kernels, filter_fields(): pl.pallas_call(lambda *refs: filter_body(in_rows, out_rows, *refs), out_s...  23.8 us
    all_to_all x4, starting transfers between devices, swap(): return lax.all_to_all(x, axes, 0, 0, tiled=True)  22.6 us
    ppermute x7, starting transfers between devices, shards(): lax.ppermute(ens[k], 'mem', [(i, (i + k) % MEMS) for i in range(MEMS)])  20.4 us
    pallas_call x1, Pallas kernels, middle(): pl.pallas_call(lambda *refs: middle_body(scale, *refs), in_specs=[pl.Bloc...  6.18 us
    pallas_call x1, Pallas kernels, spread(): pl.pallas_call(spread_body, grid_spec=pltpu.PrefetchScalarGridSpec(num_sc...  5.23 us
  transfers between devices with their start and end apart: 11, of which 6 were waited for; matrix products, arithmetic and copies ran while one was open for 1% of the time, Pallas kernels for 8%

profile of v2, /device:TPU:2, one launch (start us, length us, event | category | flops | bytes accessed | tf_op | source)
XLA Modules:
  0.0 221.6 jit_solution(18442563457144498885)
XLA Ops:
  0.6 2.8 %pack.1 = f32[2,8,25,8,128]{4,3,2,1,0:T(8,128)} custom-call(f32[2,20,64,160]{3,2,1,0:T(8,128)} %bitcast.26), custom_call_target="tpu_custom_call" | custom-call | tf_op jit(solution)/shard_map/pack/pallas_call | solution.py:93
  3.4 8.2 %all-to-all-start = ((f32[16,25,8,128]{3,2,1,0:T(8,128)}), f32[16,25,8,128]{3,2,1,0:T(8,128)S(1)}, u32[]{:S(2)}, u32[]{:S(2)}) async-start(f32[16,25,8,128]{3,2,1,0:T(8,128)} %bitcast.32), calls=%async_computation | async-start | bytes 3276800 | tf_op jit(solution)/shard_map/all_to_all | solution.py:297
  11.7 0.1 copy.9
  11.8 0.6 gather_fusion
  12.7 0.6 pad_maximum_fusion.refs_1_
  13.3 22.9 %all-to-all-done = f32[16,25,8,128]{3,2,1,0:T(8,128)S(1)} async-done(((f32[16,25,8,128]{3,2,1,0:T(8,128)}), f32[16,25,8,128]{3,2,1,0:T(8,128)S(1)}, u32[]{:S(2)}, u32[]{:S(2)}) %all-to-all-start) | async-done | bytes 1638432 | tf_op jit(solution)/shard_map/all_to_all | solution.py:297
  36.2 1.2 copy-done.1
  37.4 12.0 %filter_out.1 = f32[4096,128]{1,0:T(8,128)} custom-call(f32[3200,128]{1,0:T(8,128)} %bitcast.31, f32[8,640]{1,0:T(8,128)} %pad_maximum_fusion.refs_1_, bf16[768,640]{1,0:T(8,128)(2,1)} %constant.33.clone.refs_2_, bf16[640,1280]{1,0:T(8,128)(2,1)} %constant.32.clone.refs_3_), custom_call_target="tpu_custom_call" | custom-call | tf_op jit(solution)/shard_map/filter_out/pallas_call | solution.py:235
  49.5 6.3 %all-to-all-start.1 = ((f32[128,4,8,128]{3,2,1,0:T(8,128)}), f32[128,4,8,128]{3,2,1,0:T(8,128)S(1)}, u32[]{:S(2)}, u32[]{:S(2)}) async-start(f32[128,4,8,128]{3,2,1,0:T(8,128)} %bitcast.29), calls=%async_computation.1 | async-start | bytes 4194304 | tf_op jit(solution)/shard_map/all_to_all | solution.py:297
  55.8 5.2 %spread.1 = (f32[4,4,64,128]{3,2,1,0:T(8,128)}, f32[4,4,64,128]{3,2,1,0:T(8,128)}, f32[4,4,64,128]{3,2,1,0:T(8,128)}, f32[4,4,64,128]{3,2,1,0:T(8,128)}, f32[4,4...) custom-call(s32[1]{0:T(128)} %bitcast.me_ref.refs_0_, ...), custom_call_target="tpu_custom_call" | custom-call | tf_op jit(solution)/shard_map/spread/pallas_call | solution.py:164
  61.1 0.1 collective-permute-start
  61.2 1.5 collective-permute-start.1
  62.6 1.6 collective-permute-start.2
  64.2 1.9 collective-permute-start.3
  66.1 1.2 collective-permute-start.4
  67.2 21.9 %collective-permute-done = f32[4,4,64,128]{3,2,1,0:T(8,128)S(1)} collective-permute-done((f32[4,4,64,128]{3,2,1,0:T(8,128)}, f32[4,4,64,128]{3,2,1,0:T(8,128)S(1)}, u32[]{:S(2)}, u32[]{:S(2)}) %collective-permute-start) | collective-permute-done | bytes 524320 | tf_op jit(solution)/shard_map/ppermute | solution.py:312
  89.1 3.6 %collective-permute-start.5 = (f32[4,4,64,128]{3,2,1,0:T(8,128)}, f32[4,4,64,128]{3,2,1,0:T(8,128)}, u32[]{:S(2)}, u32[]{:S(2)}) collective-permute-start(f32[4,4,64,128]{3,2,1,0:T(8,128)} %get-tuple-element.20), channel_id=1, source_target_pairs={{0,96},{16,112},{32,0},{48,16},{64,32},{80,48},{96,64},{112,80},{1... | collective-permute-start | bytes 1572872 | tf_op jit(solution)/shard_map/ppermute | solution.py:312
  92.7 10.7 %collective-permute-start.6 = (f32[4,4,64,128]{3,2,1,0:T(8,128)}, f32[4,4,64,128]{3,2,1,0:T(8,128)}, u32[]{:S(2)}, u32[]{:S(2)}) collective-permute-start(f32[4,4,64,128]{3,2,1,0:T(8,128)} %get-tuple-element.21), channel_id=1, source_target_pairs={{0,112},{16,0},{32,16},{48,32},{64,48},{80,64},{96,80},{112,96},{1... | collective-permute-start | bytes 1572872 | tf_op jit(solution)/shard_map/ppermute | solution.py:312
  103.3 0.7 copy.11
  104.0 9.2 %collective-permute-done.4 = f32[4,4,64,128]{3,2,1,0:T(8,128)} collective-permute-done((f32[4,4,64,128]{3,2,1,0:T(8,128)}, f32[4,4,64,128]{3,2,1,0:T(8,128)}, u32[]{:S(2)}, u32[]{:S(2)}) %collective-permute-start.4) | collective-permute-done | bytes 524320 | tf_op jit(solution)/shard_map/ppermute | solution.py:312
  113.2 1.2 collective-permute-done.5
  114.5 8.7 %collective-permute-done.6 = f32[4,4,64,128]{3,2,1,0:T(8,128)} collective-permute-done((f32[4,4,64,128]{3,2,1,0:T(8,128)}, f32[4,4,64,128]{3,2,1,0:T(8,128)}, u32[]{:S(2)}, u32[]{:S(2)}) %collective-permute-start.6) | collective-permute-done | bytes 524320 | tf_op jit(solution)/shard_map/ppermute | solution.py:312
  123.2 1.3 copy-done
  124.5 6.2 %middle.1 = (f32[8,2,8,4,8,128]{5,4,3,2,1,0:T(8,128)}, f32[8,2,4,8,128]{4,3,2,1,0:T(8,128)}) custom-call(s32[1]{0:T(128)} %bitcast.me_ref.refs_0_, f32[8,2,8,4,8,128]{5,4,3,2,1,0:T(8,128)} %bitcast.28, f32[64,64]{1,0:T(8,128)} %refs_2_.3, f32[64,64]{1,0:T(8,128)} %bitcast.42, f32[2,2,4,64,128]{4,3,2,1,0:T(8,128)} %bitcast.38, ...), custom_call_target="tpu_custom_call" | custom-call | tf_op jit(solution)/shard_map/middle/pallas_call | solution.py:284
  130.7 40.7 %all_to_all.25 = f32[128,4,8,128]{3,2,1,0:T(8,128)} all-to-all(f32[128,4,8,128]{3,2,1,0:T(8,128)} %bitcast.37), channel_id=1, replica_groups=mesh['mem'=8,'tile'=16] {'mem','tile'}, dimensions={0} | all-to-all | bytes 4194304 | tf_op jit(solution)/shard_map/all_to_all | solution.py:297
  171.4 4.4 %all-to-all-start.3 = ((f32[8,2,4,8,128]{4,3,2,1,0:T(8,128)}), f32[8,2,4,8,128]{4,3,2,1,0:T(8,128)S(1)}, u32[]{:S(2)}, u32[]{:S(2)}) async-start(f32[8,2,4,8,128]{4,3,2,1,0:T(8,128)} %get-tuple-element.24), calls=%async_computation.3 | async-start | bytes 524288 | tf_op jit(solution)/shard_map/all_to_all | solution.py:297
  175.8 11.8 %filter_back.1 = f32[3200,128]{1,0:T(8,128)} custom-call(f32[4096,128]{1,0:T(8,128)} %bitcast.30, f32[8,640]{1,0:T(8,128)} %pad_maximum_fusion.refs_1_, bf16[768,640]{1,0:T(8,128)(2,1)} %constant.33.clone.refs_2_, bf16[640,1280]{1,0:T(8,128)(2,1)} %constant.32.clone.refs_3_), custom_call_target="tpu_custom_call" | custom-call | tf_op jit(solution)/shard_map/filter_back/pallas_call | solution.py:235
  187.6 3.7 %all-to-all-start.4 = ((f32[16,25,8,128]{3,2,1,0:T(8,128)}), f32[16,25,8,128]{3,2,1,0:T(8,128)S(1)}, u32[]{:S(2)}, u32[]{:S(2)}) async-start(f32[16,25,8,128]{3,2,1,0:T(8,128)} %bitcast.33), calls=%async_computation.4 | async-start | bytes 3276800 | tf_op jit(solution)/shard_map/all_to_all | solution.py:297
  191.3 1.8 unpack_wind.1
  193.1 23.9 %all-to-all-done.4 = f32[16,25,8,128]{3,2,1,0:T(8,128)S(1)} async-done(((f32[16,25,8,128]{3,2,1,0:T(8,128)}), f32[16,25,8,128]{3,2,1,0:T(8,128)S(1)}, u32[]{:S(2)}, u32[]{:S(2)}) %all-to-all-start.4) | async-done | bytes 1638432 | tf_op jit(solution)/shard_map/all_to_all | solution.py:297
  217.0 1.2 copy-done.2
  218.2 3.5 %finish.1 = f32[2,20,64,160]{3,2,1,0:T(8,128)} custom-call(f32[2,8,25,8,128]{4,3,2,1,0:T(8,128)} %bitcast.34, f32[2,20,64,160]{3,2,1,0:T(8,128)} %bitcast.27), custom_call_target="tpu_custom_call" | custom-call | tf_op jit(solution)/shard_map/finish/pallas_call | solution.py:117
  (27 shorter events, 0.4 us)
Async XLA Ops:
  3.4 8.2 %copy-start.7 = (f32[16,4]{0,1:T(4,128)S(1)}, f32[16,4]{0,1:T(4,128)}, u32[]{:S(2)}) copy-start(f32[16,4]{0,1:T(4,128)} %param.10) | copy-start | bytes 772
  3.4 8.3 %copy-start.8 = (s32[64]{0:T(128)S(1)}, s32[64]{0:T(128)}, u32[]{:S(2)}) copy-start(s32[64]{0:T(128)} %param.11) | copy-start | bytes 772
  3.4 32.8 %all-to-all-start = ((f32[16,25,8,128]{3,2,1,0:T(8,128)}), f32[16,25,8,128]{3,2,1,0:T(8,128)S(1)}, u32[]{:S(2)}, u32[]{:S(2)}) async-start(f32[16,25,8,128]{3,2,1,0:T(8,128)} %bitcast.32), calls=%async_computation | async-start | bytes 3276800 | tf_op jit(solution)/shard_map/all_to_all | solution.py:297
  36.2 1.2 copy-start.1
  49.5 73.7 %all-to-all-start.1 = ((f32[128,4,8,128]{3,2,1,0:T(8,128)}), f32[128,4,8,128]{3,2,1,0:T(8,128)S(1)}, u32[]{:S(2)}, u32[]{:S(2)}) async-start(f32[128,4,8,128]{3,2,1,0:T(8,128)} %bitcast.29), calls=%async_computation.1 | async-start | bytes 4194304 | tf_op jit(solution)/shard_map/all_to_all | solution.py:297
  55.8 47.5 %copy-start.6 = (f32[64,64]{1,0:T(8,128)S(1)}, f32[64,64]{1,0:T(8,128)}, u32[]{:S(2)}) copy-start(f32[64,64]{1,0:T(8,128)} %refs_2_.3) | copy-start | bytes 49156
  61.1 28.0 %collective-permute-start = (f32[4,4,64,128]{3,2,1,0:T(8,128)}, f32[4,4,64,128]{3,2,1,0:T(8,128)S(1)}, u32[]{:S(2)}, u32[]{:S(2)}) collective-permute-start(f32[4,4,64,128]{3,2,1,0:T(8,128)} %get-tuple-element.15), channel_id=1, source_target_pairs={{0,16},{16,32},{32,48},{48,64},{64,80},{80,96},{96,112},{112,0},{1... | collective-permute-start | bytes 1572872 | tf_op jit(solution)/shard_map/ppermute | solution.py:312
  61.2 31.5 %collective-permute-start.1 = (f32[4,4,64,128]{3,2,1,0:T(8,128)}, f32[4,4,64,128]{3,2,1,0:T(8,128)S(1)}, u32[]{:S(2)}, u32[]{:S(2)}) collective-permute-start(f32[4,4,64,128]{3,2,1,0:T(8,128)} %get-tuple-element.16), channel_id=1, source_target_pairs={{0,32},{16,48},{32,64},{48,80},{64,96},{80,112},{96,0},{112,16},{1... | collective-permute-start | bytes 1572872 | tf_op jit(solution)/shard_map/ppermute | solution.py:312
  62.6 41.4 %collective-permute-start.2 = (f32[4,4,64,128]{3,2,1,0:T(8,128)}, f32[4,4,64,128]{3,2,1,0:T(8,128)}, u32[]{:S(2)}, u32[]{:S(2)}) collective-permute-start(f32[4,4,64,128]{3,2,1,0:T(8,128)} %get-tuple-element.17), channel_id=1, source_target_pairs={{0,48},{16,64},{32,80},{48,96},{64,112},{80,0},{96,16},{112,32},{1... | collective-permute-start | bytes 1572872 | tf_op jit(solution)/shard_map/ppermute | solution.py:312
  64.2 39.8 %collective-permute-start.3 = (f32[4,4,64,128]{3,2,1,0:T(8,128)}, f32[4,4,64,128]{3,2,1,0:T(8,128)}, u32[]{:S(2)}, u32[]{:S(2)}) collective-permute-start(f32[4,4,64,128]{3,2,1,0:T(8,128)} %get-tuple-element.18), channel_id=1, source_target_pairs={{0,64},{16,80},{32,96},{48,112},{64,0},{80,16},{96,32},{112,48},{1... | collective-permute-start | bytes 1572872 | tf_op jit(solution)/shard_map/ppermute | solution.py:312
  66.1 47.2 %collective-permute-start.4 = (f32[4,4,64,128]{3,2,1,0:T(8,128)}, f32[4,4,64,128]{3,2,1,0:T(8,128)}, u32[]{:S(2)}, u32[]{:S(2)}) collective-permute-start(f32[4,4,64,128]{3,2,1,0:T(8,128)} %get-tuple-element.19), channel_id=1, source_target_pairs={{0,80},{16,96},{32,112},{48,0},{64,16},{80,32},{96,48},{112,64},{1... | collective-permute-start | bytes 1572872 | tf_op jit(solution)/shard_map/ppermute | solution.py:312
  89.1 34.1 %copy-start.4 = (f32[4,4,64,128]{3,2,1,0:T(8,128)}, f32[4,4,64,128]{3,2,1,0:T(8,128)S(1)}, u32[]{:S(2)}) copy-start(f32[4,4,64,128]{3,2,1,0:T(8,128)S(1)} %collective-permute-done) | copy-start | bytes 1572868
  89.1 25.4 %collective-permute-start.5 = (f32[4,4,64,128]{3,2,1,0:T(8,128)}, f32[4,4,64,128]{3,2,1,0:T(8,128)}, u32[]{:S(2)}, u32[]{:S(2)}) collective-permute-start(f32[4,4,64,128]{3,2,1,0:T(8,128)} %get-tuple-element.20), channel_id=1, source_target_pairs={{0,96},{16,112},{32,0},{48,16},{64,32},{80,48},{96,64},{112,80},{1... | collective-permute-start | bytes 1572872 | tf_op jit(solution)/shard_map/ppermute | solution.py:312
  92.7 30.5 %copy-start.5 = (f32[4,4,64,128]{3,2,1,0:T(8,128)}, f32[4,4,64,128]{3,2,1,0:T(8,128)S(1)}, u32[]{:S(2)}) copy-start(f32[4,4,64,128]{3,2,1,0:T(8,128)S(1)} %collective-permute-done.1) | copy-start | bytes 1572868
  92.7 30.5 %collective-permute-start.6 = (f32[4,4,64,128]{3,2,1,0:T(8,128)}, f32[4,4,64,128]{3,2,1,0:T(8,128)}, u32[]{:S(2)}, u32[]{:S(2)}) collective-permute-start(f32[4,4,64,128]{3,2,1,0:T(8,128)} %get-tuple-element.21), channel_id=1, source_target_pairs={{0,112},{16,0},{32,16},{48,32},{64,48},{80,64},{96,80},{112,96},{1... | collective-permute-start | bytes 1572872 | tf_op jit(solution)/shard_map/ppermute | solution.py:312
  123.2 1.3 copy-start
  171.4 16.2 %all-to-all-start.3 = ((f32[8,2,4,8,128]{4,3,2,1,0:T(8,128)}), f32[8,2,4,8,128]{4,3,2,1,0:T(8,128)S(1)}, u32[]{:S(2)}, u32[]{:S(2)}) async-start(f32[8,2,4,8,128]{4,3,2,1,0:T(8,128)} %get-tuple-element.24), calls=%async_computation.3 | async-start | bytes 524288 | tf_op jit(solution)/shard_map/all_to_all | solution.py:297
  187.6 3.7 %copy-start.3 = (f32[8,2,4,8,128]{4,3,2,1,0:T(8,128)}, f32[8,2,4,8,128]{4,3,2,1,0:T(8,128)S(1)}, u32[]{:S(2)}) copy-start(f32[8,2,4,8,128]{4,3,2,1,0:T(8,128)S(1)} %all-to-all-done.3.x_ref) | copy-start | bytes 786436
  187.6 29.4 %all-to-all-start.4 = ((f32[16,25,8,128]{3,2,1,0:T(8,128)}), f32[16,25,8,128]{3,2,1,0:T(8,128)S(1)}, u32[]{:S(2)}, u32[]{:S(2)}) async-start(f32[16,25,8,128]{3,2,1,0:T(8,128)} %bitcast.33), calls=%async_computation.4 | async-start | bytes 3276800 | tf_op jit(solution)/shard_map/all_to_all | solution.py:297
  217.0 1.2 copy-start.2

commit v3 on v2

v3 whole, which is shorter than its diff:
```python
import math

import jax
import jax.numpy as jnp
import ml_dtypes
import numpy as np
from jax import lax
from jax.experimental import pallas as pl
from jax.experimental.pallas import tpu as pltpu
from jax.sharding import PartitionSpec as P


DILATIONS = (1, 2, 4, 8)
TILES = 16
MEMS = 8
ROWS = 20
NX = 320
NY = 160
LV = 64
MAIN = 128
TAIL = 32
GROUPS = ROWS // 4
K = ROWS + GROUPS
FULL = K // MEMS
Q = FULL + 1
LAST = K - 1
CUT = MAIN // MEMS
SHARE = FULL * LV + LV // MEMS
FIELDS = 8
NS = len(DILATIONS)
bf16 = jnp.bfloat16
f32 = jnp.float32


def line_filter(length, dilation):
    positions = np.arange(length)
    distance = np.abs(positions[None, :] - positions[:, None])
    inside = (distance % dilation == 0) & (distance <= 6 * dilation)
    ratio = (distance // dilation).astype(np.float64)
    kernel = np.where(inside, np.exp(-ratio * ratio / 8.0), 0.0)
    cubed = kernel @ kernel @ kernel
    centre = cubed[:, length // 2]
    return cubed / np.sqrt(np.sum(centre * centre))


def split_np(a):
    hi = a.astype(np.float32).astype(ml_dtypes.bfloat16)
    lo = (a - hi.astype(np.float64)).astype(np.float32).astype(ml_dtypes.bfloat16)
    return hi, lo


def x_order():
    order = []
    for j in range(4):
        for g in range(GROUPS):
            for t in range(TILES):
                order.append(ROWS * t + 4 * g + j)
    return np.array(order)


def constants():
    order = x_order()
    gx = np.concatenate(
        [line_filter(NX, d)[order][:, order] for d in DILATIONS], axis=1
    )
    gys = [line_filter(NY, d).T for d in DILATIONS]
    gy = np.concatenate([g[:, :MAIN] for g in gys] + [g[:, MAIN:] for g in gys], axis=1)
    gy = np.concatenate([gy, np.zeros((2 * MAIN - NY, NS * NY))], axis=0)
    return split_np(gx), split_np(gy)


def split(a):
    hi = a.astype(bf16)
    lo = (a - hi.astype(f32)).astype(bf16)
    return hi, lo


def dot(a, b):
    return jnp.dot(a, b, preferred_element_type=f32)


def params(mib):
    return pltpu.CompilerParams(vmem_limit_bytes=mib * 1024 * 1024)


WHOLE = pl.BlockSpec(memory_space=pltpu.VMEM)
HBM = pl.BlockSpec(memory_space=pltpu.HBM)
SMEM = pl.BlockSpec(memory_space=pltpu.SMEM)
dma = pltpu.SemaphoreType.DMA


def in_hbm(x):
    return pltpu.with_memory_space_constraint(x, pltpu.HBM)


def main_at(r):
    return 5 * (r // 4) + r % 4


def tail_at(g):
    return 5 * g + 4


def own_cut(i, shape):
    return lax.broadcasted_iota(jnp.int32, shape, len(shape) - 1) // CUT == i


def pack_body(x_hbm, o_hbm, x_ref, o_ref, in_sems, out_sems):
    blocks = [(m, g) for m in range(x_ref.shape[0]) for g in range(GROUPS)]
    loads, stores = [], []
    for n, (m, g) in enumerate(blocks):
        rows = pl.ds(4 * g, 4)
        loads.append(pltpu.make_async_copy(x_hbm.at[m, rows], x_ref.at[m, rows], in_sems.at[n]))
        loads[-1].start()
    for n, (m, g) in enumerate(blocks):
        loads[n].wait()
        for j in range(4):
            o_ref[m, :, 5 * g + j] = x_ref[m, 4 * g + j, :, :MAIN].reshape(LV // 8, 8, MAIN)
        tails = [x_ref[m, 4 * g + j, :, MAIN:] for j in range(4)]
        o_ref[m, :, 5 * g + 4] = jnp.concatenate(tails, axis=1).reshape(LV // 8, 8, MAIN)
        part = (m, slice(None), pl.ds(5 * g, 5))
        stores.append(pltpu.make_async_copy(o_ref.at[part], o_hbm.at[part], out_sems.at[n]))
        stores[-1].start()
    for copy in stores:
        copy.wait()


def pack(x):
    n = x.shape[0]
    shape = (n, LV // 8, K, 8, MAIN)
    return pl.pallas_call(
        pack_body,
        in_specs=[HBM],
        out_specs=HBM,
        out_shape=pltpu.HBM(shape, f32),
        scratch_shapes=[
            pltpu.VMEM((n, ROWS, LV, NY), f32),
            pltpu.VMEM(shape, f32),
            dma((n * GROUPS,)),
            dma((n * GROUPS,)),
        ],
        compiler_params=params(12),
        name="pack",
    )(in_hbm(x))


def finish_body(y_ref, c_ref, o_hbm, o_ref, sems):
    stores = []
    for m in range(o_ref.shape[0]):
        for g in range(GROUPS):
            tails = y_ref[m, :, 5 * g + 4].reshape(LV, MAIN)
            for j in range(4):
                r = 4 * g + j
                main = y_ref[m, :, 5 * g + j].reshape(LV, MAIN)
                o_ref[m, r, :, :MAIN] = c_ref[m, r, :, :MAIN] + main
                tail = tails[:, TAIL * j : TAIL * (j + 1)]
                o_ref[m, r, :, MAIN:] = c_ref[m, r, :, MAIN:] + tail
            part = (m, pl.ds(4 * g, 4))
            n = len(stores)
            stores.append(pltpu.make_async_copy(o_ref.at[part], o_hbm.at[part], sems.at[n]))
            stores[-1].start()
    for copy in stores:
        copy.wait()


def finish(y, control):
    n = y.shape[0]
    shape = (n, ROWS, LV, NY)
    return pl.pallas_call(
        finish_body,
        in_specs=[WHOLE, WHOLE],
        out_specs=HBM,
        out_shape=jax.ShapeDtypeStruct(shape, f32),
        scratch_shapes=[pltpu.VMEM(shape, f32), dma((n * GROUPS,))],
        compiler_params=params(12),
        name="finish",
    )(y, control)


def unpack_wind_body(me_ref, *refs):
    got_refs, o_ref, x_ref = refs[:MEMS], refs[MEMS], refs[MEMS + 1]
    for k in range(MEMS):
        x_ref[lax.rem(me_ref[0] + MEMS - k, MEMS)] = got_refs[k][...]
    for c in range(2):
        last = x_ref[0, c, FULL]
        for i in range(1, MEMS):
            last = jnp.where(own_cut(i, last.shape), x_ref[i, c, FULL], last)
        for r in range(ROWS):
            k = main_at(r)
            o_ref[c, r, :, :MAIN] = x_ref[k % MEMS, c, k // MEMS]
        for g in range(GROUPS):
            k = tail_at(g)
            tails = last if k == LAST else x_ref[k % MEMS, c, k // MEMS]
            for j in range(4):
                o_ref[c, 4 * g + j, :, MAIN:] = tails[:, TAIL * j : TAIL * (j + 1)]


def unpack_wind(me, got):
    return pl.pallas_call(
        unpack_wind_body,
        in_specs=[SMEM] + [WHOLE] * MEMS,
        out_shape=jax.ShapeDtypeStruct((2, ROWS, LV // MEMS, NY), f32),
        scratch_shapes=[pltpu.VMEM((MEMS, 2, Q, LV // MEMS, MAIN), f32)],
        compiler_params=params(8),
        name="unpack_wind",
    )(me, *got)


def spread_body(me_ref, x_ref, *refs):
    o_refs, packed = refs[:MEMS], refs[MEMS]

    def keep(k, value):
        packed[k % MEMS, LV * (k // MEMS) : LV * (k // MEMS + 1)] = value

    for r in range(ROWS):
        keep(main_at(r), x_ref[0, r, :, :MAIN])
    for g in range(GROUPS):
        tails = jnp.concatenate([x_ref[0, 4 * g + j, :, MAIN:] for j in range(4)], axis=1)
        if tail_at(g) != LAST:
            keep(tail_at(g), tails)
    tiles = [tails[8 * u : 8 * (u + 1)] for u in range(LV // 8)]
    for d in range(MEMS):
        joined = pltpu.roll(tiles[0], CUT * (-d % MEMS), 1) if d else tiles[0]
        for u in range(1, LV // 8):
            shift = (u - d) % MEMS
            moved = pltpu.roll(tiles[u], CUT * shift, 1) if shift else tiles[u]
            joined = jnp.where(own_cut(u, joined.shape), moved, joined)
        packed[d, FULL * LV :] = joined
    for k in range(MEMS):
        o_refs[k][0] = packed[lax.rem(me_ref[0] + k, MEMS)]


def spread(me, x):
    n = x.shape[0]
    return pl.pallas_call(
        spread_body,
        grid_spec=pltpu.PrefetchScalarGridSpec(
            num_scalar_prefetch=1,
            grid=(n,),
            in_specs=[pl.BlockSpec((1, ROWS, LV, NY), lambda i, me: (i, 0, 0, 0))],
            out_specs=[pl.BlockSpec((1, SHARE, MAIN), lambda i, me: (i, 0, 0))] * MEMS,
            scratch_shapes=[pltpu.VMEM((MEMS, SHARE, MAIN), f32)],
        ),
        out_shape=[pltpu.HBM((n, SHARE, MAIN), f32)] * MEMS,
        compiler_params=params(12),
        name="spread",
    )(me, in_hbm(x))


def field_rows(k, f):
    return pl.ds(8 * k + f, TILES, stride=8 * K)


def share_rows(i, q, f):
    return pl.ds((i * TILES * Q + q) * 8 + f, TILES, stride=8 * Q)


def load_tile(ref, shared, k, f):
    if not shared:
        return ref[field_rows(k, f), :]
    if k != LAST:
        return ref[share_rows(k % MEMS, k // MEMS, f), :]
    value = ref[share_rows(0, FULL, f), :]
    for i in range(1, MEMS):
        value = jnp.where(own_cut(i, value.shape), ref[share_rows(i, FULL, f), :], value)
    return value


def store_tile(ref, shared, k, f, value):
    if not shared:
        ref[field_rows(k, f), :] = value
    elif k != LAST:
        ref[share_rows(k % MEMS, k // MEMS, f), :] = value
    else:
        for i in range(MEMS):
            ref[share_rows(i, FULL, f), :] = value


def filter_body(
    out_shared, x_ref, w_ref, gy_hbm, gx_hbm, o_hbm, lhs_ref, gy_ref, gx_ref, hi_ref, lo_ref, o_ref, sems
):
    wide = 2 * MAIN
    parts = ((0, 0), (0, wide), (wide, 2 * wide))
    copies = [
        pltpu.make_async_copy(gy_hbm.at[pl.ds(a, wide)], gy_ref.at[pl.ds(b, wide)], sems.at[n])
        for n, (a, b) in enumerate(parts)
    ]
    copies.append(pltpu.make_async_copy(gx_hbm, gx_ref, sems.at[3]))
    for copy in copies:
        copy.start()
    span = TILES * GROUPS
    count = span * FIELDS

    def put(j, f, g, at, value):
        hi, lo = split(value)
        rows = slice(count * j + span * f + TILES * g, count * j + span * f + TILES * (g + 1))
        lhs_ref[rows, at : at + MAIN] = hi
        lhs_ref[rows, wide + at : wide + at + MAIN] = lo
        lhs_ref[rows, 2 * wide + at : 2 * wide + at + MAIN] = hi

    for f in range(FIELDS):
        for g in range(GROUPS):
            tail = load_tile(x_ref, not out_shared, tail_at(g), f)
            for j in range(4):
                moved = pltpu.roll(tail, MAIN - TAIL * j, 1) if j else tail
                put(j, f, g, MAIN, moved)
                put(j, f, g, 0, load_tile(x_ref, not out_shared, main_at(4 * g + j), f))
    for copy in copies[:3]:
        copy.wait()
    for j in range(4):
        y = dot(lhs_ref[count * j : count * (j + 1), :], gy_ref[...])
        fields = [y[span * f : span * (f + 1)] * w_ref[f : f + 1, :] for f in range(FIELDS)]
        for s in range(NS):
            at = s * NX + j * span
            pieces = [fields[f][:, MAIN * s : MAIN * (s + 1)] for f in range(FIELDS)]
            for q in range(FIELDS // 4):
                lane = NS * MAIN + TAIL * s
                pieces.append(
                    jnp.concatenate(
                        [fields[4 * q + i][:, lane : lane + TAIL] for i in range(4)], axis=1
                    )
                )
            hi, lo = split(jnp.concatenate(pieces, axis=1))
            hi_ref[at : at + span, :] = hi
            lo_ref[at : at + span, :] = lo
    copies[3].wait()
    both = dot(gx_ref[...], hi_ref[...])
    out = both[:NX] + both[NX:] + dot(gx_ref[:NX, :], lo_ref[...])

    def result(k, f):
        g, j = k // 5, k % 5
        at = [TILES * (GROUPS * i + g) for i in range(4)]
        if j < 4:
            return out[at[j] : at[j] + TILES, MAIN * f : MAIN * (f + 1)]
        lane = FIELDS * MAIN + MAIN * (f // 4) + TAIL * (f % 4)
        return jnp.concatenate([out[a : a + TILES, lane : lane + TAIL] for a in at], axis=1)

    if out_shared:
        rows = TILES * Q * FIELDS
        batches = [[LAST]] + [[i + MEMS * q for q in range(FULL)] for i in range(MEMS)]
    else:
        batches = [[5 * g + j for j in range(5)] for g in range(GROUPS)]
    stores = []
    for n, batch in enumerate(batches):
        for k in batch:
            for f in range(FIELDS):
                store_tile(o_ref, out_shared, k, f, result(k, f))
        sem = sems.at[4 + len(stores)]
        if out_shared and n:
            part = pl.ds(rows * (n - 1), rows)
            stores.append(pltpu.make_async_copy(o_ref.at[part], o_hbm.at[part], sem))
            stores[-1].start()
        elif not out_shared and n == len(batches) - 1:
            stores.append(pltpu.make_async_copy(o_ref, o_hbm, sem))
            stores[-1].start()
    for copy in stores:
        copy.wait()


def filter_fields(x, w, gy, gx, out_shared):
    rows = TILES * FIELDS * (MEMS * Q if out_shared else K)
    return pl.pallas_call(
        lambda *refs: filter_body(out_shared, *refs),
        in_specs=[WHOLE, WHOLE, HBM, HBM],
        out_specs=HBM,
        out_shape=pltpu.HBM((rows, MAIN), f32),
        scratch_shapes=[
            pltpu.VMEM((FIELDS * NX, 6 * MAIN), bf16),
            pltpu.VMEM((6 * MAIN, NS * NY), bf16),
            pltpu.VMEM((2 * NX, NS * NX), bf16),
            pltpu.VMEM((NS * NX, FIELDS * NY), bf16),
            pltpu.VMEM((NS * NX, FIELDS * NY), bf16),
            pltpu.VMEM((rows, MAIN), f32),
            dma((4 + MEMS,)),
        ],
        compiler_params=params(36),
        name="filter_out" if out_shared else "filter_back",
    )(x, w, in_hbm(gy), in_hbm(gx))


def mix(v, x):
    hi, lo = split(x)
    return dot(v[0], hi) + dot(v[0], lo) + dot(v[1], hi)


def middle_body(scale, me_ref, x_ref, v_ref, vt_ref, *refs):
    e_refs, o_ref, wind_refs = refs[:MEMS], refs[MEMS], refs[MEMS + 1 : 2 * MEMS + 1]
    cut_ref, wind_ref = refs[2 * MEMS + 1 :]
    v, vt = split(v_ref[...]), split(vt_ref[...])
    me = me_ref[0]
    wind = [None, None]
    for k in range(MEMS):
        at = lax.rem(me + MEMS - k, MEMS)
        for m in range(2):
            tiles = [x_ref[at, m, :, q].reshape(LV, MAIN) for q in range(Q)]
            loc = mix(v, jnp.concatenate(tiles, axis=1))
            for c in range(2):
                joined = e_refs[k][m, c, FULL * LV :]
                for u in range(LV // 8):
                    moved = pltpu.roll(joined, CUT * lax.rem(me + MEMS - u, MEMS), 1)
                    cut_ref[k, m, c, 8 * u : 8 * (u + 1)] = moved
                tiles = [e_refs[k][m, c, LV * q : LV * (q + 1)] for q in range(FULL)]
                ens = jnp.concatenate(tiles + [cut_ref[k, m, c]], axis=1)
                wind[c] = ens * loc if wind[c] is None else wind[c] + ens * loc
    wind = [w * scale for w in wind]
    for c in range(2):
        for q in range(Q):
            tile = wind[c][:, MAIN * q : MAIN * (q + 1)]
            wind_ref[:, c, q] = tile.reshape(MEMS, LV // MEMS, MAIN)
    for k in range(MEMS):
        wind_refs[k][...] = wind_ref[lax.rem(me + k, MEMS)]
    for k in range(MEMS):
        at = lax.rem(me + MEMS - k, MEMS)
        for m in range(2):
            adj = None
            for c in range(2):
                tiles = [e_refs[k][m, c, LV * q : LV * (q + 1)] for q in range(FULL)]
                ens = jnp.concatenate(tiles + [cut_ref[k, m, c]], axis=1)
                adj = ens * wind[c] if adj is None else adj + ens * wind[c]
            back = mix(vt, adj * scale)
            for q in range(Q):
                tile = back[:, MAIN * q : MAIN * (q + 1)]
                o_ref[at, m, :, q] = tile.reshape(LV // 8, 8, MAIN)


def middle(me, x, v, ens, scale):
    return pl.pallas_call(
        lambda *refs: middle_body(scale, *refs),
        in_specs=[SMEM] + [WHOLE] * (3 + MEMS),
        out_specs=[WHOLE] * (1 + MEMS),
        out_shape=[jax.ShapeDtypeStruct((MEMS, 2, LV // 8, Q, 8, MAIN), f32)]
        + [jax.ShapeDtypeStruct((2, Q, LV // MEMS, MAIN), f32)] * MEMS,
        scratch_shapes=[
            pltpu.VMEM((MEMS, 2, 2, LV, MAIN), f32),
            pltpu.VMEM((MEMS, 2, Q, LV // MEMS, MAIN), f32),
        ],
        compiler_params=params(24),
        name="middle",
    )(me, x, v, v.T, *ens)


def swap(x, axes):
    return lax.all_to_all(x, axes, 0, 0, tiled=True)


def shards(control, ens_perts, vert_corr, slab_wts, level_slab):
    members = control.shape[0]
    scale = 1.0 / math.sqrt(members * MEMS - 1)
    (gxh, gxl), (gyh, gyl) = constants()

    control = jnp.transpose(control, (0, 2, 1, 3))
    got = swap(pack(control).reshape(TILES, K, FIELDS, MAIN), "tile")

    me = lax.axis_index("mem").reshape(1)
    ens = jnp.transpose(ens_perts, (0, 1, 3, 2, 4)).reshape(4, ROWS, LV, NY)
    ens = list(spread(me, ens))
    for k in range(1, MEMS):
        ens[k] = lax.ppermute(ens[k], "mem", [(i, (i + k) % MEMS) for i in range(MEMS)])
    ens = [e.reshape(2, 2, SHARE, MAIN) for e in ens]

    gx = jnp.asarray(np.concatenate([gxh, gxl], axis=0))
    gy = jnp.asarray(np.concatenate([gyh, gyl], axis=0))
    level_wts = slab_wts[level_slab]
    first = FIELDS * (lax.axis_index("tile") % (LV // FIELDS))
    own = lax.dynamic_slice_in_dim(level_wts, first, FIELDS, 0)
    w = jnp.concatenate([jnp.repeat(own, MAIN, axis=1), jnp.repeat(own, TAIL, axis=1)], axis=1)

    smooth = filter_fields(got.reshape(TILES * K * FIELDS, MAIN), w, gy, gx, True)
    got = swap(smooth.reshape(MEMS * TILES, Q, FIELDS, MAIN), ("mem", "tile"))
    got = got.reshape(MEMS, 2, LV // 8, Q, 8, MAIN)
    adj, *wind = middle(me, got, vert_corr, ens, scale)
    got = swap(adj.reshape(MEMS * TILES, Q, FIELDS, MAIN), ("mem", "tile"))
    smooth = filter_fields(got.reshape(MEMS * TILES * Q * FIELDS, MAIN), w, gy, gx, False)
    smooth, wind = lax.optimization_barrier((smooth, wind))
    got = swap(smooth.reshape(TILES, K, FIELDS, MAIN), "tile")
    for k in range(1, MEMS):
        wind[k] = lax.ppermute(wind[k], "mem", [(i, (i + k) % MEMS) for i in range(MEMS)])
    wind = unpack_wind(me, wind)
    gradient = finish(got.reshape(2, LV // 8, K, 8, MAIN), control)
    return (jnp.transpose(wind, (0, 2, 1, 3)), jnp.transpose(gradient, (0, 2, 1, 3)))


def solution(mesh):
    return jax.shard_map(
        shards,
        mesh=mesh,
        in_specs=(P("mem", None, "tile", None), P("mem", None, None, "tile", None), P(), P(), P()),
        out_specs=(P(None, "mem", "tile", None), P("mem", None, "tile", None)),
        check_vma=False,
    )
```

time: 222 us -> 201 us (0.905)
  the two profiles are of different devices: /device:TPU:2 before, /device:TPU:0 now
where the time goes in v3:
time: 201 us
  waiting for transfers between devices  75.3 us (37%)
  starting transfers between devices  42.6 us (21%)
  blocking collectives  41.1 us (20%)
  Pallas kernels  38.6 us (19%)
  local copies, waits for them, and re-layouts  2.12 us (1%)
    all_to_all x1, blocking collectives, swap(): return lax.all_to_all(x, axes, 0, 0, tiled=True)  41.1 us
    all_to_all x3, waiting for transfers between devices, swap(): return lax.all_to_all(x, axes, 0, 0, tiled=True)  36.5 us
    ppermute x7, waiting for transfers between devices, shards(): lax.ppermute(ens[k], 'mem', [(i, (i + k) % MEMS) for i in range(MEMS)])  35.6 us
    pallas_call x2, Pallas kernels, filter_fields(): pl.pallas_call(lambda *refs: filter_body(out_shared, *refs), in_specs=[WH...  23.2 us
    all_to_all x3, starting transfers between devices, swap(): return lax.all_to_all(x, axes, 0, 0, tiled=True)  19.7 us
    ppermute x7, starting transfers between devices, shards(): lax.ppermute(ens[k], 'mem', [(i, (i + k) % MEMS) for i in range(MEMS)])  15.9 us
    ppermute x7, starting transfers between devices, shards(): lax.ppermute(wind[k], 'mem', [(i, (i + k) % MEMS) for i in range(MEMS)])  6.94 us
    pallas_call x1, Pallas kernels, spread(): pl.pallas_call(spread_body, grid_spec=pltpu.PrefetchScalarGridSpec(num_sc...  5.26 us
  transfers between devices with their start and end apart: 17, of which 10 were waited for; matrix products, arithmetic and copies ran while one was open for 1% of the time, Pallas kernels for 3%

profile of v3, /device:TPU:0, one launch (start us, length us, event | category | flops | bytes accessed | tf_op | source)
XLA Modules:
  0.0 200.8 jit_solution(8495745257565210919)
XLA Ops:
  0.6 2.7 %pack.1 = f32[2,8,25,8,128]{4,3,2,1,0:T(8,128)} custom-call(f32[2,20,64,160]{3,2,1,0:T(8,128)} %bitcast.26), custom_call_target="tpu_custom_call" | custom-call | tf_op jit(solution)/shard_map/pack/pallas_call | solution.py:131
  3.4 8.2 %all-to-all-start = ((f32[16,25,8,128]{3,2,1,0:T(8,128)}), f32[16,25,8,128]{3,2,1,0:T(8,128)S(1)}, u32[]{:S(2)}, u32[]{:S(2)}) async-start(f32[16,25,8,128]{3,2,1,0:T(8,128)} %bitcast.39), calls=%async_computation | async-start | bytes 3276800 | tf_op jit(solution)/shard_map/all_to_all | solution.py:443
  11.7 0.6 gather_fusion
  12.6 23.5 %all-to-all-done = f32[16,25,8,128]{3,2,1,0:T(8,128)S(1)} async-done(((f32[16,25,8,128]{3,2,1,0:T(8,128)}), f32[16,25,8,128]{3,2,1,0:T(8,128)S(1)}, u32[]{:S(2)}, u32[]{:S(2)}) %all-to-all-start) | async-done | bytes 1638432 | tf_op jit(solution)/shard_map/all_to_all | solution.py:443
  36.2 11.9 %filter_out.1 = f32[4096,128]{1,0:T(8,128)} custom-call(f32[3200,128]{1,0:T(8,128)S(1)} %bitcast.30, f32[8,640]{1,0:T(8,128)S(1)} %pad_maximum_fusion.refs_1_, bf16[512,640]{1,0:T(8,128)(2,1)} %constant.33.clone.refs_2_, bf16[640,1280]{1,0:T(8,128)(2,1)} %constant.32.clone.refs_3_), custom_call_target="tpu_custom_call" | custom-call | tf_op jit(solution)/shard_map/filter_out/pallas_call | solution.py:362
  48.0 6.9 %all-to-all-start.1 = ((f32[128,4,8,128]{3,2,1,0:T(8,128)}), f32[128,4,8,128]{3,2,1,0:T(8,128)S(1)}, u32[]{:S(2)}, u32[]{:S(2)}) async-start(f32[128,4,8,128]{3,2,1,0:T(8,128)} %bitcast.37), calls=%async_computation.1 | async-start | bytes 4194304 | tf_op jit(solution)/shard_map/all_to_all | solution.py:443
  54.9 5.3 %spread.1 = (f32[4,200,128]{2,1,0:T(8,128)}, f32[4,200,128]{2,1,0:T(8,128)}, f32[4,200,128]{2,1,0:T(8,128)}, f32[4,200,128]{2,1,0:T(8,128)}, f32[4,200,128]{2,1,...) custom-call(s32[1]{0:T(128)} %bitcast.me_ref.refs_0_, f32[4,20,64,160]{3,2,1,0:T(8,128)} %bitcast.40), custom_call_target="tpu_custom_call" | custom-call | tf_op jit(solution)/shard_map/spread/pallas_call | solution.py:235
  60.2 1.1 collective-permute-start.1
  61.3 2.0 collective-permute-start.2
  63.2 2.1 %collective-permute-start.3 = (f32[4,200,128]{2,1,0:T(8,128)}, f32[4,200,128]{2,1,0:T(8,128)}, u32[]{:S(2)}, u32[]{:S(2)}) collective-permute-start(f32[4,200,128]{2,1,0:T(8,128)} %get-tuple-element.32), channel_id=1, source_target_pairs={{0,64},{16,80},{32,96},{48,112},{64,0},{80,16},{96,32},{112,48},{1... | collective-permute-start | bytes 1228808 | tf_op jit(solution)/shard_map/ppermute | solution.py:458
  65.3 1.6 collective-permute-start.4
  66.9 21.3 %collective-permute-done = f32[4,200,128]{2,1,0:T(8,128)S(1)} collective-permute-done((f32[4,200,128]{2,1,0:T(8,128)}, f32[4,200,128]{2,1,0:T(8,128)S(1)}, u32[]{:S(2)}, u32[]{:S(2)}) %collective-permute-start) | collective-permute-done | bytes 409632 | tf_op jit(solution)/shard_map/ppermute | solution.py:458
  88.3 0.7 collective-permute-start.5
  89.1 8.5 %collective-permute-start.6 = (f32[4,200,128]{2,1,0:T(8,128)}, f32[4,200,128]{2,1,0:T(8,128)}, u32[]{:S(2)}, u32[]{:S(2)}) collective-permute-start(f32[4,200,128]{2,1,0:T(8,128)} %get-tuple-element.35), channel_id=1, source_target_pairs={{0,112},{16,0},{32,16},{48,32},{64,48},{80,64},{96,80},{112,96},{1... | collective-permute-start | bytes 1228808 | tf_op jit(solution)/shard_map/ppermute | solution.py:458
  97.6 8.3 %collective-permute-done.2 = f32[4,200,128]{2,1,0:T(8,128)S(1)} collective-permute-done((f32[4,200,128]{2,1,0:T(8,128)}, f32[4,200,128]{2,1,0:T(8,128)S(1)}, u32[]{:S(2)}, u32[]{:S(2)}) %collective-permute-start.2) | collective-permute-done | bytes 409632 | tf_op jit(solution)/shard_map/ppermute | solution.py:458
  105.9 1.3 collective-permute-done.3
  107.2 4.6 %collective-permute-done.4 = f32[4,200,128]{2,1,0:T(8,128)} collective-permute-done((f32[4,200,128]{2,1,0:T(8,128)}, f32[4,200,128]{2,1,0:T(8,128)}, u32[]{:S(2)}, u32[]{:S(2)}) %collective-permute-start.4) | collective-permute-done | bytes 409632 | tf_op jit(solution)/shard_map/ppermute | solution.py:458
  111.8 1.0 copy-done.1
  112.8 3.5 %middle.1 = (f32[8,2,8,4,8,128]{5,4,3,2,1,0:T(8,128)S(1)}, f32[2,4,8,128]{3,2,1,0:T(8,128)S(1)}, f32[2,4,8,128]{3,2,1,0:T(8,128)S(1)}, f32[2,4,8,128]{3,2,1,0:T(...) custom-call(s32[1]{0:T(128)} %bitcast.me_ref.refs_0_, ...), custom_call_target="tpu_custom_call" | custom-call | tf_op jit(solution)/shard_map/middle/pallas_call | solution.py:427
  116.3 41.1 %all_to_all.20 = f32[128,4,8,128]{3,2,1,0:T(8,128)S(1)} all-to-all(f32[128,4,8,128]{3,2,1,0:T(8,128)S(1)} %bitcast.31), channel_id=1, replica_groups=mesh['mem'=8,'tile'=16] {'mem','tile'}, dimensions={0} | all-to-all | bytes 4194304 | tf_op jit(solution)/shard_map/all_to_all | solution.py:443
  157.4 11.4 %filter_back.1 = f32[3200,128]{1,0:T(8,128)} custom-call(f32[4096,128]{1,0:T(8,128)S(1)} %bitcast.29, f32[8,640]{1,0:T(8,128)S(1)} %pad_maximum_fusion.refs_1_, bf16[512,640]{1,0:T(8,128)(2,1)} %constant.33.clone.refs_2_, bf16[640,1280]{1,0:T(8,128)(2,1)} %constant.32.clone.refs_3_), custom_call_target="tpu_custom_call" | custom-call | tf_op jit(solution)/shard_map/filter_back/pallas_call | solution.py:362
  168.8 4.7 %all-to-all-start.3 = ((f32[16,25,8,128]{3,2,1,0:T(8,128)}), f32[16,25,8,128]{3,2,1,0:T(8,128)}, u32[]{:S(2)}, u32[]{:S(2)}) async-start(f32[16,25,8,128]{3,2,1,0:T(8,128)} %bitcast.38), calls=%async_computation.3 | async-start | bytes 3276800 | tf_op jit(solution)/shard_map/all_to_all | solution.py:443
  173.6 1.0 collective-permute-start.8
  174.6 1.3 collective-permute-start.9
  175.9 2.7 %collective-permute-start.10 = (f32[2,4,8,128]{3,2,1,0:T(8,128)S(1)}, f32[2,4,8,128]{3,2,1,0:T(8,128)S(1)}, u32[]{:S(2)}, u32[]{:S(2)}) collective-permute-start(f32[2,4,8,128]{3,2,1,0:T(8,128)S(1)} %copy-done.4), channel_id=1, source_target_pairs={{0,64},{16,80},{32,96},{48,112},{64,0},{80,16},{96,32},{112,48},{1... | collective-permute-start | bytes 98312 | tf_op jit(solution)/shard_map/ppermute | solution.py:477
  178.6 1.0 collective-permute-start.11
  179.6 0.9 collective-permute-start.12
  180.5 1.0 collective-permute-done.10.refs_4_
  182.0 1.8 collective-permute-done.12.refs_6_
  183.8 0.8 unpack_wind.1
  184.6 12.9 %all-to-all-done.3 = f32[16,25,8,128]{3,2,1,0:T(8,128)} async-done(((f32[16,25,8,128]{3,2,1,0:T(8,128)}), f32[16,25,8,128]{3,2,1,0:T(8,128)}, u32[]{:S(2)}, u32[]{:S(2)}) %all-to-all-start.3) | async-done | bytes 1638432 | tf_op jit(solution)/shard_map/all_to_all | solution.py:443
  197.5 3.1 %finish.1 = f32[2,20,64,160]{3,2,1,0:T(8,128)} custom-call(f32[2,8,25,8,128]{4,3,2,1,0:T(8,128)} %bitcast.22.y_ref, f32[2,20,64,160]{3,2,1,0:T(8,128)S(1)} %bitcast.27), custom_call_target="tpu_custom_call" | custom-call | tf_op jit(solution)/shard_map/finish/pallas_call | solution.py:169
  (47 shorter events, 1.1 us)
Async XLA Ops:
  3.4 8.2 %copy-start.11 = (f32[16,4]{0,1:T(4,128)S(1)}, f32[16,4]{0,1:T(4,128)}, u32[]{:S(2)}) copy-start(f32[16,4]{0,1:T(4,128)} %param.10) | copy-start | bytes 772
  3.4 8.3 %copy-start.12 = (s32[64]{0:T(128)S(1)}, s32[64]{0:T(128)}, u32[]{:S(2)}) copy-start(s32[64]{0:T(128)} %param.11) | copy-start | bytes 772
  3.4 32.8 %all-to-all-start = ((f32[16,25,8,128]{3,2,1,0:T(8,128)}), f32[16,25,8,128]{3,2,1,0:T(8,128)S(1)}, u32[]{:S(2)}, u32[]{:S(2)}) async-start(f32[16,25,8,128]{3,2,1,0:T(8,128)} %bitcast.39), calls=%async_computation | async-start | bytes 3276800 | tf_op jit(solution)/shard_map/all_to_all | solution.py:443
  48.0 63.8 %all-to-all-start.1 = ((f32[128,4,8,128]{3,2,1,0:T(8,128)}), f32[128,4,8,128]{3,2,1,0:T(8,128)S(1)}, u32[]{:S(2)}, u32[]{:S(2)}) async-start(f32[128,4,8,128]{3,2,1,0:T(8,128)} %bitcast.37), calls=%async_computation.1 | async-start | bytes 4194304 | tf_op jit(solution)/shard_map/all_to_all | solution.py:443
  54.9 42.6 %copy-start.2 = (f32[64,64]{1,0:T(8,128)S(1)}, f32[64,64]{1,0:T(8,128)}, u32[]{:S(2)}) copy-start(f32[64,64]{1,0:T(8,128)} %refs_2_.3) | copy-start | bytes 49156
  60.2 28.0 %collective-permute-start = (f32[4,200,128]{2,1,0:T(8,128)}, f32[4,200,128]{2,1,0:T(8,128)S(1)}, u32[]{:S(2)}, u32[]{:S(2)}) collective-permute-start(f32[4,200,128]{2,1,0:T(8,128)} %get-tuple-element.29), channel_id=1, source_target_pairs={{0,16},{16,32},{32,48},{48,64},{64,80},{80,96},{96,112},{112,0},{1... | collective-permute-start | bytes 1228808 | tf_op jit(solution)/shard_map/ppermute | solution.py:458
  60.2 28.8 %collective-permute-start.1 = (f32[4,200,128]{2,1,0:T(8,128)}, f32[4,200,128]{2,1,0:T(8,128)S(1)}, u32[]{:S(2)}, u32[]{:S(2)}) collective-permute-start(f32[4,200,128]{2,1,0:T(8,128)} %get-tuple-element.30), channel_id=1, source_target_pairs={{0,32},{16,48},{32,64},{48,80},{64,96},{80,112},{96,0},{112,16},{1... | collective-permute-start | bytes 1228808 | tf_op jit(solution)/shard_map/ppermute | solution.py:458
  61.3 44.6 %collective-permute-start.2 = (f32[4,200,128]{2,1,0:T(8,128)}, f32[4,200,128]{2,1,0:T(8,128)S(1)}, u32[]{:S(2)}, u32[]{:S(2)}) collective-permute-start(f32[4,200,128]{2,1,0:T(8,128)} %get-tuple-element.31), channel_id=1, source_target_pairs={{0,48},{16,64},{32,80},{48,96},{64,112},{80,0},{96,16},{112,32},{1... | collective-permute-start | bytes 1228808 | tf_op jit(solution)/shard_map/ppermute | solution.py:458
  63.2 43.9 %collective-permute-start.3 = (f32[4,200,128]{2,1,0:T(8,128)}, f32[4,200,128]{2,1,0:T(8,128)}, u32[]{:S(2)}, u32[]{:S(2)}) collective-permute-start(f32[4,200,128]{2,1,0:T(8,128)} %get-tuple-element.32), channel_id=1, source_target_pairs={{0,64},{16,80},{32,96},{48,112},{64,0},{80,16},{96,32},{112,48},{1... | collective-permute-start | bytes 1228808 | tf_op jit(solution)/shard_map/ppermute | solution.py:458
  65.3 46.5 %collective-permute-start.4 = (f32[4,200,128]{2,1,0:T(8,128)}, f32[4,200,128]{2,1,0:T(8,128)}, u32[]{:S(2)}, u32[]{:S(2)}) collective-permute-start(f32[4,200,128]{2,1,0:T(8,128)} %get-tuple-element.33), channel_id=1, source_target_pairs={{0,80},{16,96},{32,112},{48,0},{64,16},{80,32},{96,48},{112,64},{1... | collective-permute-start | bytes 1228808 | tf_op jit(solution)/shard_map/ppermute | solution.py:458
  88.3 23.5 %collective-permute-start.5 = (f32[4,200,128]{2,1,0:T(8,128)}, f32[4,200,128]{2,1,0:T(8,128)}, u32[]{:S(2)}, u32[]{:S(2)}) collective-permute-start(f32[4,200,128]{2,1,0:T(8,128)} %get-tuple-element.34), channel_id=1, source_target_pairs={{0,96},{16,112},{32,0},{48,16},{64,32},{80,48},{96,64},{112,80},{1... | collective-permute-start | bytes 1228808 | tf_op jit(solution)/shard_map/ppermute | solution.py:458
  89.1 22.7 %collective-permute-start.6 = (f32[4,200,128]{2,1,0:T(8,128)}, f32[4,200,128]{2,1,0:T(8,128)}, u32[]{:S(2)}, u32[]{:S(2)}) collective-permute-start(f32[4,200,128]{2,1,0:T(8,128)} %get-tuple-element.35), channel_id=1, source_target_pairs={{0,112},{16,0},{32,16},{48,32},{64,48},{80,64},{96,80},{112,96},{1... | collective-permute-start | bytes 1228808 | tf_op jit(solution)/shard_map/ppermute | solution.py:458
  111.8 1.0 copy-start.1
  116.3 41.1 %copy-start.3 = (f32[2,4,8,128]{3,2,1,0:T(8,128)}, f32[2,4,8,128]{3,2,1,0:T(8,128)S(1)}, u32[]{:S(2)}) copy-start(f32[2,4,8,128]{3,2,1,0:T(8,128)S(1)} %get-tuple-element.49) | copy-start | bytes 98308
  116.3 41.1 %copy-start.5 = (f32[2,4,8,128]{3,2,1,0:T(8,128)}, f32[2,4,8,128]{3,2,1,0:T(8,128)S(1)}, u32[]{:S(2)}) copy-start(f32[2,4,8,128]{3,2,1,0:T(8,128)S(1)} %get-tuple-element.48) | copy-start | bytes 98308
  116.3 41.1 %copy-start.7 = (f32[2,4,8,128]{3,2,1,0:T(8,128)}, f32[2,4,8,128]{3,2,1,0:T(8,128)S(1)}, u32[]{:S(2)}) copy-start(f32[2,4,8,128]{3,2,1,0:T(8,128)S(1)} %get-tuple-element.47) | copy-start | bytes 98308
  116.3 41.1 %copy-start.9 = (f32[2,4,8,128]{3,2,1,0:T(8,128)}, f32[2,4,8,128]{3,2,1,0:T(8,128)S(1)}, u32[]{:S(2)}) copy-start(f32[2,4,8,128]{3,2,1,0:T(8,128)S(1)} %get-tuple-element.46) | copy-start | bytes 98308
  168.8 4.8 %copy-start.10 = (f32[2,4,8,128]{3,2,1,0:T(8,128)S(1)}, f32[2,4,8,128]{3,2,1,0:T(8,128)}, u32[]{:S(2)}) copy-start(f32[2,4,8,128]{3,2,1,0:T(8,128)} %copy-done.9) | copy-start | bytes 98308
  168.8 4.8 %copy-start.8 = (f32[2,4,8,128]{3,2,1,0:T(8,128)S(1)}, f32[2,4,8,128]{3,2,1,0:T(8,128)}, u32[]{:S(2)}) copy-start(f32[2,4,8,128]{3,2,1,0:T(8,128)} %copy-done.7) | copy-start | bytes 98308
  168.8 5.8 %copy-start.6 = (f32[2,4,8,128]{3,2,1,0:T(8,128)S(1)}, f32[2,4,8,128]{3,2,1,0:T(8,128)}, u32[]{:S(2)}) copy-start(f32[2,4,8,128]{3,2,1,0:T(8,128)} %copy-done.5) | copy-start | bytes 98308
  168.8 7.1 %copy-start.4 = (f32[2,4,8,128]{3,2,1,0:T(8,128)S(1)}, f32[2,4,8,128]{3,2,1,0:T(8,128)}, u32[]{:S(2)}) copy-start(f32[2,4,8,128]{3,2,1,0:T(8,128)} %copy-done.3) | copy-start | bytes 98308
  168.8 28.7 %copy-start = (f32[2,64,20,160]{3,1,2,0:T(8,128)S(1)}, f32[2,64,20,160]{3,1,2,0:T(8,128)}, u32[]{:S(2)}) copy-start(f32[2,64,20,160]{3,1,2,0:T(8,128)} %param.7) | copy-start | bytes 4915204
  168.8 28.7 %all-to-all-start.3 = ((f32[16,25,8,128]{3,2,1,0:T(8,128)}), f32[16,25,8,128]{3,2,1,0:T(8,128)}, u32[]{:S(2)}, u32[]{:S(2)}) async-start(f32[16,25,8,128]{3,2,1,0:T(8,128)} %bitcast.38), calls=%async_computation.3 | async-start | bytes 3276800 | tf_op jit(solution)/shard_map/all_to_all | solution.py:443
  173.5 6.1 %collective-permute-start.7 = (f32[2,4,8,128]{3,2,1,0:T(8,128)S(1)}, f32[2,4,8,128]{3,2,1,0:T(8,128)S(1)}, u32[]{:S(2)}, u32[]{:S(2)}) collective-permute-start(f32[2,4,8,128]{3,2,1,0:T(8,128)S(1)} %copy-done.10), channel_id=1, source_target_pairs={{0,16},{16,32},{32,48},{48,64},{64,80},{80,96},{96,112},{112,0},{1... | collective-permute-start | bytes 98312 | tf_op jit(solution)/shard_map/ppermute | solution.py:477
  173.6 6.9 %collective-permute-start.8 = (f32[2,4,8,128]{3,2,1,0:T(8,128)S(1)}, f32[2,4,8,128]{3,2,1,0:T(8,128)S(1)}, u32[]{:S(2)}, u32[]{:S(2)}) collective-permute-start(f32[2,4,8,128]{3,2,1,0:T(8,128)S(1)} %copy-done.8), channel_id=1, source_target_pairs={{0,32},{16,48},{32,64},{48,80},{64,96},{80,112},{96,0},{112,16},{1... | collective-permute-start | bytes 98312 | tf_op jit(solution)/shard_map/ppermute | solution.py:477
  174.6 5.9 %collective-permute-start.9 = (f32[2,4,8,128]{3,2,1,0:T(8,128)S(1)}, f32[2,4,8,128]{3,2,1,0:T(8,128)S(1)}, u32[]{:S(2)}, u32[]{:S(2)}) collective-permute-start(f32[2,4,8,128]{3,2,1,0:T(8,128)S(1)} %copy-done.6), channel_id=1, source_target_pairs={{0,48},{16,64},{32,80},{48,96},{64,112},{80,0},{96,16},{112,32},{1... | collective-permute-start | bytes 98312 | tf_op jit(solution)/shard_map/ppermute | solution.py:477
  175.9 5.6 %collective-permute-start.10 = (f32[2,4,8,128]{3,2,1,0:T(8,128)S(1)}, f32[2,4,8,128]{3,2,1,0:T(8,128)S(1)}, u32[]{:S(2)}, u32[]{:S(2)}) collective-permute-start(f32[2,4,8,128]{3,2,1,0:T(8,128)S(1)} %copy-done.4), channel_id=1, source_target_pairs={{0,64},{16,80},{32,96},{48,112},{64,0},{80,16},{96,32},{112,48},{1... | collective-permute-start | bytes 98312 | tf_op jit(solution)/shard_map/ppermute | solution.py:477
  178.6 3.3 %collective-permute-start.11 = (f32[2,4,8,128]{3,2,1,0:T(8,128)S(1)}, f32[2,4,8,128]{3,2,1,0:T(8,128)S(1)}, u32[]{:S(2)}, u32[]{:S(2)}) collective-permute-start(f32[2,4,8,128]{3,2,1,0:T(8,128)S(1)} %get-tuple-element.50), channel_id=1, source_target_pairs={{0,80},{16,96},{32,112},{48,0},{64,16},{80,32},{96,48},{112,64},{1... | collective-permute-start | bytes 98312 | tf_op jit(solution)/shard_map/ppermute | solution.py:477
  179.6 4.2 %collective-permute-start.12 = (f32[2,4,8,128]{3,2,1,0:T(8,128)S(1)}, f32[2,4,8,128]{3,2,1,0:T(8,128)S(1)}, u32[]{:S(2)}, u32[]{:S(2)}) collective-permute-start(f32[2,4,8,128]{3,2,1,0:T(8,128)S(1)} %get-tuple-element.51), channel_id=1, source_target_pairs={{0,96},{16,112},{32,0},{48,16},{64,32},{80,48},{96,64},{112,80},{1... | collective-permute-start | bytes 98312 | tf_op jit(solution)/shard_map/ppermute | solution.py:477
  180.5 3.2 %collective-permute-start.13 = (f32[2,4,8,128]{3,2,1,0:T(8,128)S(1)}, f32[2,4,8,128]{3,2,1,0:T(8,128)S(1)}, u32[]{:S(2)}, u32[]{:S(2)}) collective-permute-start(f32[2,4,8,128]{3,2,1,0:T(8,128)S(1)} %get-tuple-element.52), channel_id=1, source_target_pairs={{0,112},{16,0},{32,16},{48,32},{64,48},{80,64},{96,80},{112,96},{1... | collective-permute-start | bytes 98312 | tf_op jit(solution)/shard_map/ppermute | solution.py:477
